TPU v7x, 256 devices: a whole 4x4x8 slice. The times are simulated.
256 devices in a mesh: face: 16 (over x_hi, y, core), band: 16 (over z, x_lo).
Axes of the slice: x: 4 (x_hi: 2, x_lo: 2; x = x_hi * 2 + x_lo), y: 4, z: 8, core: 2. Of those that a mesh axis runs over, the one named last changes fastest.
Arguments:
- coarse: bfloat16 [192, 256, 256], P('band', 'face'), may hold values from -6 to 6
- skip: bfloat16 [384, 512, 256], P('band', 'face'), may hold values from -6 to 6
- up_weight: bfloat16 [3, 3, 256, 256], replicated, may hold values from -0.25 to 0.25
- conv_weight: bfloat16 [3, 3, 256, 256], replicated, may hold values from -0.125 to 0.125
- cotangent: bfloat16 [384, 512, 256], P('band', 'face'), may hold values from -6 to 6
Outputs:
- decoded: bfloat16 [384, 512, 256], P('band', 'face')
- grad_coarse: bfloat16 [192, 256, 256], P('band', 'face')
- grad_up_weight: float32 [2304, 256], P('face', 'band')
- grad_conv_weight: float32 [2304, 256], P('face', 'band')
All inputs are finite; a program needn't handle non-finite values.
Results may differ from a plain program's by a relative error of at most 0.0049.
Values may be sent and summed in bfloat16 or wider, within the bound.
A program may use at most 128 MiB of HBM per device.

v0:
```python
import jax
import jax.numpy as jnp
from jax import lax
from jax.sharding import PartitionSpec as P

forward_taps = ((1, 1), (0, 0), (1, 0))
backward_taps = ((1, 0), (0, 1), (1, 1))


def with_halo(x, sides, width, wrap):
    for axis, dim in sides:
        count, length = (lax.axis_size(axis), x.shape[dim])
        up = [(i, (i + 1) % count) for i in range(count if wrap else count - 1)]
        down = [(j, i) for i, j in up]
        last = lax.slice_in_dim(x, length - width, length, axis=dim)
        first = lax.slice_in_dim(x, 0, width, axis=dim)
        before = lax.ppermute(last, axis, up)
        after = lax.ppermute(first, axis, down)
        x = jnp.concatenate([before, x, after], axis=dim)
    return x


def from_behind(block, axis, distance):
    devices = range(lax.axis_size(axis))
    route = [((i - distance) % len(devices), i) for i in devices]
    return lax.ppermute(block, axis, route)


def from_behind_2(block, axis, distance):
    devices = range(lax.axis_size(axis))
    route = [(i - distance, i) for i in devices if i - distance in devices]
    return lax.ppermute(block, axis, route)


def up_phases(extended, up_weight, n_rows, n_cols):
    channels = extended.shape[-1]
    totals = {}
    for row_tap in range(3):
        row_phase, row_off = forward_taps[row_tap]
        for col_tap in range(3):
            col_phase, col_off = forward_taps[col_tap]
            source = extended[row_off : row_off + n_rows, col_off : col_off + n_cols].reshape(
                -1, channels
            )
            term = jnp.dot(source, up_weight[row_tap, col_tap], preferred_element_type=jnp.float32)
            name = (row_phase, col_phase)
            totals[name] = totals[name] + term if name in totals else term
    per_row = []
    for row_phase in range(2):
        per_row.append(
            jnp.stack(
                [
                    totals[row_phase, col_phase].reshape(n_rows, n_cols, channels)
                    for col_phase in range(2)
                ],
                axis=2,
            )
        )
    return jnp.stack(per_row, axis=1)


def conv_forward(act_pad, conv_weight, n_rows, n_cols):
    channels = act_pad.shape[-1]
    total = jnp.zeros((n_rows * n_cols, channels), jnp.float32)
    for row_tap in range(3):
        for col_tap in range(3):
            source = act_pad[row_tap : row_tap + n_rows, col_tap : col_tap + n_cols].reshape(
                -1, channels
            )
            total = total + jnp.dot(
                source, conv_weight[row_tap, col_tap], preferred_element_type=jnp.float32
            )
    return total


def conv_backward(grad_pad, conv_weight, n_rows, n_cols):
    channels = grad_pad.shape[-1]
    total = jnp.zeros((n_rows * n_cols, channels), jnp.float32)
    for row_tap in range(3):
        for col_tap in range(3):
            source = grad_pad[
                2 - row_tap : 2 - row_tap + n_rows, 2 - col_tap : 2 - col_tap + n_cols
            ].reshape(-1, channels)
            total = total + jnp.dot(
                source, conv_weight[row_tap, col_tap].T, preferred_element_type=jnp.float32
            )
    return total


def conv_wgrad(act_pad, grad_flat, n_rows, n_cols):
    channels = act_pad.shape[-1]
    blocks = []
    for row_tap in range(3):
        for col_tap in range(3):
            source = act_pad[row_tap : row_tap + n_rows, col_tap : col_tap + n_cols].reshape(
                -1, channels
            )
            blocks.append(jnp.dot(source.T, grad_flat, preferred_element_type=jnp.float32))
    return jnp.concatenate(blocks, axis=0)


def down_backward(grad_ext, coarse, up_weight, n_rows, n_cols):
    channels = coarse.shape[-1]
    coarse_flat = coarse.reshape(-1, channels)
    grad_in = jnp.zeros((n_rows * n_cols, channels), jnp.float32)
    blocks = []
    for row_tap in range(3):
        row_phase, row_start = backward_taps[row_tap]
        for col_tap in range(3):
            col_phase, col_start = backward_taps[col_tap]
            source = grad_ext[
                row_start : row_start + n_rows, row_phase, col_start : col_start + n_cols, col_phase
            ].reshape(-1, channels)
            grad_in = grad_in + jnp.dot(
                source, up_weight[row_tap, col_tap].T, preferred_element_type=jnp.float32
            )
            blocks.append(jnp.dot(coarse_flat.T, source, preferred_element_type=jnp.float32))
    return (grad_in, jnp.concatenate(blocks, axis=0))


def fine_halo(field):
    beside_all = with_halo(field, (("face", 1),), 1, True)
    return with_halo(beside_all, (("band", 0),), 1, False)


def local(coarse, skip, up_weight, conv_weight, cotangent):
    n_rows, n_cols, channels = coarse.shape
    padded = jnp.pad(coarse, ((1, 1), (1, 1), (0, 0)))
    spread = up_phases(padded, up_weight, n_rows + 1, n_cols + 1)
    col_part = from_behind(spread[:, :, :1, 1:], "face", -1)
    spread = spread.at[:, :, n_cols:, 1:].add(col_part)
    spread = spread[:, :, 1:]
    row_part = from_behind_2(spread[:1, 1:], "band", -1)
    spread = spread.at[n_rows:, 1:].add(row_part)
    upsampled = spread[1:]
    preact = upsampled.reshape(2 * n_rows, 2 * n_cols, channels) + skip.astype(jnp.float32)
    act = jax.nn.silu(preact).astype(jnp.bfloat16)
    act_pad = fine_halo(act)
    decoded = conv_forward(act_pad, conv_weight, 2 * n_rows, 2 * n_cols)
    decoded = decoded.reshape(2 * n_rows, 2 * n_cols, channels).astype(jnp.bfloat16)
    grad_pad = fine_halo(cotangent)
    grad_act = conv_backward(grad_pad, conv_weight, 2 * n_rows, 2 * n_cols).reshape(
        2 * n_rows, 2 * n_cols, channels
    )
    sigma = jax.nn.sigmoid(preact)
    grad_pre = (grad_act * sigma * (1.0 + preact * (1.0 - sigma))).astype(jnp.bfloat16)
    phased = grad_pre.reshape(n_rows, 2, n_cols, 2, channels)
    col_prev = from_behind(phased[:, :, n_cols - 1 :, 1:], "face", 1)
    col_full = jnp.pad(col_prev, ((0, 0), (0, 0), (0, 0), (1, 0), (0, 0)))
    widened_grad = jnp.concatenate([col_full, phased], axis=2)
    row_prev = from_behind_2(widened_grad[n_rows - 1 :, 1:], "band", 1)
    row_full = jnp.pad(row_prev, ((0, 0), (1, 0), (0, 0), (0, 0), (0, 0)))
    grad_ext = jnp.concatenate([row_full, widened_grad], axis=0)
    grad_in, grad_up = down_backward(grad_ext, coarse, up_weight, n_rows, n_cols)
    grad_conv = conv_wgrad(act_pad, cotangent.reshape(-1, channels), 2 * n_rows, 2 * n_cols)
    grad_coarse = grad_in.reshape(n_rows, n_cols, channels).astype(jnp.bfloat16)
    face_parts = (
        lax.psum_scatter(grad_up, "face", scatter_dimension=0, tiled=True),
        lax.psum_scatter(grad_conv, "face", scatter_dimension=0, tiled=True),
    )
    owned_up, owned_conv = (
        lax.psum_scatter(face_parts[0], "band", scatter_dimension=1, tiled=True),
        lax.psum_scatter(face_parts[1], "band", scatter_dimension=1, tiled=True),
    )
    return (decoded, grad_coarse, owned_up, owned_conv)


def solution(mesh):
    return jax.shard_map(
        local,
        mesh=mesh,
        in_specs=(
            P("band", "face", None),
            P("band", "face", None),
            P(),
            P(),
            P("band", "face", None),
        ),
        out_specs=(
            P("band", "face", None),
            P("band", "face", None),
            P("face", "band"),
            P("face", "band"),
        ),
        check_vma=False,
    )
```

profile of v0, /device:TPU:8, one launch (start us, length us, event | category | flops | bytes accessed | tf_op | source)
XLA Modules:
  0.0 385.1 jit_solution(10357744808049872141)
XLA Ops:
  7.2 1.2 pad_slice_fusion.7
  10.9 0.9 copy-done.1
  12.0 1.7 collective-permute-start.7
  13.7 1.2 fusion.37
  15.3 1.3 collective-permute-start.8
  16.6 4.5 %collective-permute-start.9 = (bf16[1,34,256]{2,1,0:T(8,128)(2,1)S(1)}, bf16[1,34,256]{2,1,0:T(8,128)(2,1)S(1)}, u32[]{:S(2)}, u32[]{:S(2)}) collective-permute-start(bf16[1,34,256]{2,1,0:T(8,128)(2,1)S(1)} %get-tuple-element.62), channel_id=1, source_target_pairs={{0,1},{1,2},{2,3},{3,4},{4,5},{5,6},{6,7},{7,8},{8,9},{9,10},{10,1... | collective-permute-start | bytes 52232 | tf_op jit(solution)/shard_map/ppermute | solution.py:17
  21.1 1.0 pad_maximum_fusion.3
  22.5 1.3 collective-permute-start.1
  27.8 1.2 convolution_add_fusion
  29.7 1.4 reshape.208
  31.1 1.8 multiply_convert_fusion
  33.0 1.2 collective-permute-start.2
  34.2 1.1 collective-permute-start.3
  35.3 1.4 collective-permute-done.2
  36.8 4.5 %collective-permute-start.4 = (bf16[1,34,256]{2,1,0:T(8,128)(2,1)S(1)}, bf16[1,34,256]{2,1,0:T(8,128)(2,1)S(1)}, u32[]{:S(2)}, u32[]{:S(2)}) collective-permute-start(bf16[1,34,256]{2,1,0:T(8,128)(2,1)S(1)} %get-tuple-element.65), channel_id=1, source_target_pairs={{0,1},{1,2},{2,3},{3,4},{4,5},{5,6},{6,7},{7,8},{8,9},{9,10},{10,1... | collective-permute-start | bytes 52232 | tf_op jit(solution)/shard_map/ppermute | solution.py:17
  41.3 1.5 collective-permute-start.5
  43.1 4.8 %collective-permute-done.5 = bf16[1,34,256]{2,1,0:T(8,128)(2,1)S(1)} collective-permute-done((bf16[1,34,256]{2,1,0:T(8,128)(2,1)S(1)}, bf16[1,34,256]{2,1,0:T(8,128)(2,1)S(1)}, u32[]{:S(2)}, u32[]{:S(2)}) %collective-permute-start.5) | collective-permute-done | bytes 17440 | tf_op jit(solution)/shard_map/ppermute | solution.py:18
  48.2 1.0 fusion.14
  49.3 1.0 fusion.13
  50.3 1.0 fusion.12
  51.3 1.0 fusion.11
  52.3 1.0 fusion.10
  53.3 1.0 fusion.9
  54.3 1.0 fusion.8
  55.3 1.0 fusion.7
  56.3 1.0 fusion.6
  58.2 1.2 fusion.39
  59.4 3.5 collective-permute-done.10
  63.0 4.5 %collective-permute-start.11 = (bf16[1,1,17,2,256]{4,2,0,3,1:T(8,128)(2,1)S(1)}, bf16[1,1,17,2,256]{4,2,0,3,1:T(8,128)(2,1)S(1)}, u32[]{:S(2)}, u32[]{:S(2)}) collective-permute-start(bf16[1,1,17,2,256]{4,2,0,3,1:T(8,128)(2,1)S(1)} %pad_maximum_fusion.9), channel_id=1, source_target_pairs={{0,1},{1,2},{2,3},{3,4},{4,5},{5,6},{6,7},{7,8},{8,9},{9,10},{10,1... | collective-permute-start | bytes 52232 | tf_op jit(solution)/shard_map/ppermute | solution.py:32
  67.7 1.4 collective-permute-done.11
  69.4 1.1 fusion.57
  70.5 0.9 fusion.23
  79.0 1.1 convolution_add_fusion.24
  80.1 1.1 convolution_add_fusion.23
  81.2 1.1 convolution_add_fusion.22
  82.3 1.1 convolution_add_fusion.21
  83.5 1.1 convolution_add_fusion.20
  84.6 1.8 convolution_add_fusion.19
  86.9 1.0 fusion.121
  91.0 60.2 %reduce-scatter.11.cloned.1.call-done = f32[144,256]{1,0:T(8,128)} async-done(((f32[2304,256]{1,0:T(8,128)}), f32[144,256]{1,0:T(8,128)}) %reduce-scatter.11.cloned.1.call-update) | async-done | bytes 147472 | tf_op jit(solution)/shard_map/reduce_scatter | solution.py:159
  151.1 1.8 copy.31
  153.0 1.8 convolution_add_fusion.18
  155.1 80.1 %reduce-scatter.9.cloned.1.call-done = f32[144,256]{1,0:T(8,128)} async-done(((f32[2304,256]{1,0:T(8,128)}), f32[144,256]{1,0:T(8,128)}) %reduce-scatter.9.cloned.1.call-update) | async-done | bytes 147472 | tf_op jit(solution)/shard_map/reduce_scatter | solution.py:158
  235.1 1.7 copy.29
  236.9 1.9 fusion.24
  238.7 1.0 fusion.5
  239.8 67.8 %reduce-scatter.15.cloned.1.call-done = f32[16,144]{1,0:T(8,128)} async-done(((f32[256,144]{1,0:T(8,128)}), f32[16,144]{1,0:T(8,128)}) %reduce-scatter.15.cloned.1.call-update) | async-done | bytes 9232
  307.5 71.1 %reduce-scatter.13.cloned.1.call-done = f32[16,144]{1,0:T(8,128)} async-done(((f32[256,144]{1,0:T(8,128)}), f32[16,144]{1,0:T(8,128)}) %reduce-scatter.13.cloned.1.call-update) | async-done | bytes 9232
  (109 shorter events, 21.3 us)
Async XLA Ops:
  7.2 1.4 copy-start
  7.2 1.5 copy-start.3
  7.2 143.9 %reduce-scatter.11.cloned.1.call-start = ((), (), s32[]{:S(2)}) async-start(), calls=%async_computation.5 | async-start | bytes 2506752 | tf_op jit(solution)/shard_map/reduce_scatter | solution.py:159
  10.6 3.1 copy-start.2
  10.8 1.1 copy-start.1
  10.8 11.3 %collective-permute-start = (f32[13,2,1,1,256]{4,2,0,3,1:T(1,128)S(1)}, f32[13,2,1,1,256]{4,2,0,3,1:T(1,128)S(1)}, u32[]{:S(2)}, u32[]{:S(2)}) collective-permute-start(f32[13,2,1,1,256]{4,2,0,3,1:T(1,128)S(1)} %fusion.110), channel_id=1, source_target_pairs={{16,0},{32,16},{48,32},{64,48},{80,64},{96,80},{112,96},{128,112},... | collective-permute-start | bytes 79880 | tf_op jit(solution)/shard_map/ppermute | solution.py:26
  11.9 3.3 collective-permute-start.6
  12.0 3.3 collective-permute-start.7
  15.3 8.5 %collective-permute-start.8 = (bf16[1,34,256]{2,1,0:T(8,128)(2,1)S(1)}, bf16[1,34,256]{2,1,0:T(8,128)(2,1)S(1)}, u32[]{:S(2)}, u32[]{:S(2)}) collective-permute-start(bf16[1,34,256]{2,1,0:T(8,128)(2,1)S(1)} %get-tuple-element.61), channel_id=1, source_target_pairs={{1,0},{2,1},{3,2},{4,3},{5,4},{6,5},{7,6},{8,7},{9,8},{10,9},{11,1... | collective-permute-start | bytes 52232 | tf_op jit(solution)/shard_map/ppermute | solution.py:18
  16.6 7.2 %collective-permute-start.9 = (bf16[1,34,256]{2,1,0:T(8,128)(2,1)S(1)}, bf16[1,34,256]{2,1,0:T(8,128)(2,1)S(1)}, u32[]{:S(2)}, u32[]{:S(2)}) collective-permute-start(bf16[1,34,256]{2,1,0:T(8,128)(2,1)S(1)} %get-tuple-element.62), channel_id=1, source_target_pairs={{0,1},{1,2},{2,3},{3,4},{4,5},{5,6},{6,7},{7,8},{8,9},{9,10},{10,1... | collective-permute-start | bytes 52232 | tf_op jit(solution)/shard_map/ppermute | solution.py:17
  22.5 6.5 %collective-permute-start.1 = (f32[1,1,16,2,256]{4,2,0,3,1:T(8,128)S(1)}, f32[1,1,16,2,256]{4,2,0,3,1:T(8,128)S(1)}, u32[]{:S(2)}, u32[]{:S(2)}) collective-permute-start(f32[1,1,16,2,256]{4,2,0,3,1:T(8,128)S(1)} %slice.381), channel_id=1, source_target_pairs={{1,0},{2,1},{3,2},{4,3},{5,4},{6,5},{7,6},{8,7},{9,8},{10,9},{11,1... | collective-permute-start | bytes 98312 | tf_op jit(solution)/shard_map/ppermute | solution.py:32
  25.6 1.1 copy-start.5
  25.6 1.2 copy-start.11
  33.0 3.7 collective-permute-start.2
  34.2 2.6 collective-permute-start.3
  36.8 6.3 %collective-permute-start.4 = (bf16[1,34,256]{2,1,0:T(8,128)(2,1)S(1)}, bf16[1,34,256]{2,1,0:T(8,128)(2,1)S(1)}, u32[]{:S(2)}, u32[]{:S(2)}) collective-permute-start(bf16[1,34,256]{2,1,0:T(8,128)(2,1)S(1)} %get-tuple-element.65), channel_id=1, source_target_pairs={{0,1},{1,2},{2,3},{3,4},{4,5},{5,6},{6,7},{7,8},{8,9},{9,10},{10,1... | collective-permute-start | bytes 52232 | tf_op jit(solution)/shard_map/ppermute | solution.py:17
  41.3 6.6 %collective-permute-start.5 = (bf16[1,34,256]{2,1,0:T(8,128)(2,1)S(1)}, bf16[1,34,256]{2,1,0:T(8,128)(2,1)S(1)}, u32[]{:S(2)}, u32[]{:S(2)}) collective-permute-start(bf16[1,34,256]{2,1,0:T(8,128)(2,1)S(1)} %get-tuple-element.66), channel_id=1, source_target_pairs={{1,0},{2,1},{3,2},{4,3},{5,4},{6,5},{7,6},{8,7},{9,8},{10,9},{11,1... | collective-permute-start | bytes 52232 | tf_op jit(solution)/shard_map/ppermute | solution.py:18
  43.1 8.2 %copy-start.9 = (bf16[24,32,256]{2,1,0:T(8,128)(2,1)}, bf16[24,32,256]{2,1,0:T(8,128)(2,1)S(1)}, u32[]{:S(2)}) copy-start(bf16[24,32,256]{2,1,0:T(8,128)(2,1)S(1)} %get-tuple-element.78) | copy-start | bytes 1179652
  43.1 10.2 %copy-start.7 = (bf16[24,32,256]{2,1,0:T(8,128)(2,1)}, bf16[24,32,256]{2,1,0:T(8,128)(2,1)S(1)}, u32[]{:S(2)}) copy-start(bf16[24,32,256]{2,1,0:T(8,128)(2,1)S(1)} %get-tuple-element.77) | copy-start | bytes 1179652
  57.3 177.8 %reduce-scatter.9.cloned.1.call-start = ((), (), s32[]{:S(2)}) async-start(), calls=%async_computation.4 | async-start | bytes 2506752 | tf_op jit(solution)/shard_map/reduce_scatter | solution.py:158
  57.6 5.3 %collective-permute-start.10 = (bf16[12,2,1,1,256]{4,2,0,3,1:T(2,128)(2,1)S(1)}, bf16[12,2,1,1,256]{4,2,0,3,1:T(2,128)(2,1)S(1)}, u32[]{:S(2)}, u32[]{:S(2)}) collective-permute-start(bf16[12,2,1,1,256]{4,2,0,3,1:T(2,128)(2,1)S(1)} %slice.397), channel_id=1, source_target_pairs={{240,0},{0,16},{16,32},{32,48},{48,64},{64,80},{80,96},{96,112},{1... | collective-permute-start | bytes 36872 | tf_op jit(solution)/shard_map/ppermute | solution.py:26
  63.0 6.0 %collective-permute-start.11 = (bf16[1,1,17,2,256]{4,2,0,3,1:T(8,128)(2,1)S(1)}, bf16[1,1,17,2,256]{4,2,0,3,1:T(8,128)(2,1)S(1)}, u32[]{:S(2)}, u32[]{:S(2)}) collective-permute-start(bf16[1,1,17,2,256]{4,2,0,3,1:T(8,128)(2,1)S(1)} %pad_maximum_fusion.9), channel_id=1, source_target_pairs={{0,1},{1,2},{2,3},{3,4},{4,5},{5,6},{6,7},{7,8},{8,9},{9,10},{10,1... | collective-permute-start | bytes 52232 | tf_op jit(solution)/shard_map/ppermute | solution.py:32
  78.9 228.6 %reduce-scatter.15.cloned.1.call-start = ((), (), s32[]{:S(2)}) async-start(), calls=%async_computation.7 | async-start | bytes 278528
  88.4 1.1 copy-start.4
  88.4 1.3 copy-start.10
  89.7 1.0 copy-start.8
  90.7 62.3 %copy-start.12 = (f32[192,256]{1,0:T(8,128)S(1)}, f32[192,256]{1,0:T(8,128)}, u32[]{:S(2)}) copy-start(f32[192,256]{1,0:T(8,128)} %convolution_add_fusion.19) | copy-start | bytes 589828
  152.9 225.7 %reduce-scatter.13.cloned.1.call-start = ((), (), s32[]{:S(2)}) async-start(), calls=%async_computation.6 | async-start | bytes 278528
  155.0 83.7 %copy-start.6 = (bf16[24,32,256]{2,1,0:T(8,128)(2,1)S(1)}, bf16[24,32,256]{2,1,0:T(8,128)(2,1)}, u32[]{:S(2)}) copy-start(bf16[24,32,256]{2,1,0:T(8,128)(2,1)} %get-tuple-element.51) | copy-start | bytes 1179652
Sparse Core Ops, SparseCore 0:
  57.5 93.6 reduce-scatter.10
  156.0 79.0 reduce-scatter.8
  238.2 69.2 reduce-scatter.14
  310.6 67.9 reduce-scatter.12
where the time goes:
time: 386 us; the launch traced here: 385 us
  waiting for transfers between devices  291 us (75%)
  matrix products  39.7 us (10%)
  starting transfers between devices  22.6 us (6%)
  between operations  14.4 us (4%)
  local copies, waits for them, and re-layouts  13.4 us (3%)
  other arithmetic  4.54 us (1%)
    unnamed x6, waiting for transfers between devices  139 us
    reduce_scatter x1, waiting for transfers between devices, local(): lax.psum_scatter(grad_up, 'face', scatter_dimension=0, tiled=True)  80.1 us
    reduce_scatter x1, waiting for transfers between devices, local(): lax.psum_scatter(grad_conv, 'face', scatter_dimension=0, tiled=True)  60.2 us
    dot_general x9, matrix products, down_backward(): jnp.dot(source, up_weight[row_tap, col_tap].T, preferred_element_type=jnp...  12.1 us
    ppermute x4, starting transfers between devices, with_halo(): before = lax.ppermute(last, axis, up)  10.3 us
    dot_general x9, matrix products, conv_wgrad(): jnp.dot(source.T, grad_flat, preferred_element_type=jnp.float32)  9.07 us
    dot_general x9, matrix products, down_backward(): jnp.dot(coarse_flat.T, source, preferred_element_type=jnp.float32)  8.37 us
  transfers between devices with their start and end apart: 16, of which 10 were waited for; matrix products, arithmetic and copies ran while one was open for 10% of the time, Pallas kernels for 0%

commit v1 on v0

v1 whole, which is shorter than its diff:
```python
import functools

import jax
import jax.numpy as jnp
from jax import lax
from jax.experimental import pallas as pl
from jax.experimental.pallas import tpu as pltpu
from jax.sharding import PartitionSpec as P

F32, BF16 = jnp.float32, jnp.bfloat16
MESH = pl.DeviceIdType.MESH
CH = 256
RI, CJ = 12, 16
XR, XC = 18, 32
AREA = XR * XC

MSG_UP = (0, 1, 2, 5, 6)
MSG_DOWN = (0, 3, 4, 5, 6, 7, 8)
MSG_LEFT = (0, 1, 3, 5, 7)
MSG_RIGHT = (0, 2, 4, 5, 6, 7, 8)
CORNERS = (
    (-1, -1, (0, 1, 5)),
    (-1, 1, (0, 2, 5, 6)),
    (1, -1, (0, 3, 5, 7)),
    (1, 1, (0, 4, 5, 6, 7, 8)),
)
TAPS = [(k, l) for k in range(3) for l in range(3)]


def split(e):
    return e % 2, e // 2


def dot(a, b):
    return jnp.dot(a, b, preferred_element_type=F32)


def ld(ref, at, n, stride=1):
    if stride == 1:
        return jnp.concatenate([ref[h, pl.ds(at, n), :] for h in range(2)], axis=-1)
    return jnp.concatenate([ref[h, pl.ds(at, n, stride=stride), :] for h in range(2)], axis=-1)


def st(ref, at, n, value, stride=1):
    for h in range(2):
        part = value[:, 128 * h : 128 * h + 128]
        if stride == 1:
            ref[h, pl.ds(at, n), :] = part
        else:
            ref[h, pl.ds(at, n, stride=stride), :] = part


def kernel(
    dims,
    coarse_h, skip_h, upw_h, convw_h, cot_h,
    dec_h, gc_h, gu_o, gw_o,
    coarse_v, skip_v, cot_v, upw, convw, upwt, convwt,
    xf, fs, ft, af, gf, dfac, ce, tv, tvp, av, gv, actt, dec_v, gc_v,
    m_up, m_dn, m_lf, m_rt, m_co, r_bot, r_top, r_rt, r_lf, r_co,
    gsum, r0, s1, r1c, r1u, a1c, a1u, s2c, s2u, r2c, r2u, pad, a3, s3, r3,
    in_sem, out_sem, hs, hr, s0s, s0r, s1s, s1r, s2s, s2r, s3s, s3r,
):
    XH, Y, Z, XL = dims
    NX = XH * XL
    HL = CH // XL
    FB = 9 * CH // (XH * Y * 2)
    CB = CH // (Z * XL)
    nface, nband = XH * Y * 2, Z * XL
    face, band = lax.axis_index("face"), lax.axis_index("band")
    core = face % 2
    yy = (face // 2) % Y
    xh = face // (2 * Y)
    xl = band % XL
    zz = band // XL
    xx = xh * XL + xl

    def dev(xx_, yy_, core_, zz_):
        return {
            "face": (xx_ // XL) * (2 * Y) + yy_ * 2 + core_,
            "band": zz_ * XL + xx_ % XL,
        }

    def near(di, dj):
        return {"face": (face + dj + nface) % nface, "band": (band + di + nband) % nband}

    def at_core():
        return dev(xx, yy, 1 - core, zz)

    def at_y(d):
        return dev(xx, (yy + d) % Y, core, zz)

    def at_x(d):
        return dev((xx + d) % NX, yy, core, zz)

    def at_z(d):
        return dev(xx, yy, core, (zz + d) % Z)

    ways = [(-1, 0), (1, 0), (0, -1), (0, 1), (-1, -1), (-1, 1), (1, -1), (1, 1)]
    partners = [near(*w) for w in ways] + [at_core()]
    partners += [at_y(d) for d in range(1, Y)] + [at_x(d) for d in range(1, NX)]
    partners += [at_z(d) for d in range(1, Z)]
    barrier = pltpu.get_barrier_semaphore()
    for p in partners:
        pl.semaphore_signal(barrier, inc=1, device_id=p, device_id_type=MESH)

    loads = [
        pltpu.make_async_copy(src, dst, in_sem.at[n])
        for n, (src, dst) in enumerate(
            ((coarse_h, coarse_v), (skip_h, skip_v), (cot_h, cot_v), (convw_h, convw), (upw_h, upw))
        )
    ]
    for c in loads:
        c.start()

    def rows(a, i, col, n):
        return ld(xf, a * AREA + (i + 2) * XC + 8 + col, n, XC)

    for c in loads[:3]:
        c.wait()

    def spread(i, carry):
        base = pl.multiple_of((i + 2) * XC + 8, 8)
        st(xf, base, CJ, coarse_v[i].astype(F32))
        for src, stage, first in ((skip_v, fs, 1), (cot_v, ft, 5)):
            for r in range(2):
                st(stage, r * 2 * CJ, 2 * CJ, src[2 * i + r].astype(F32))
            for r in range(2):
                for s in range(2):
                    part = ld(stage, r * 2 * CJ + s, CJ, 2)
                    st(xf, pl.multiple_of(base + (first + 2 * r + s) * AREA, 8), CJ, part)
        return carry

    lax.fori_loop(0, RI, spread, 0)

    for n, a in enumerate(MSG_UP):
        m_up[n] = ld(xf, a * AREA + 2 * XC + 8, CJ).astype(BF16)
    for n, a in enumerate(MSG_DOWN):
        m_dn[n] = ld(xf, a * AREA + (RI + 1) * XC + 8, CJ).astype(BF16)
    for n, a in enumerate(MSG_LEFT):
        m_lf[n] = rows(a, 0, 0, 16).astype(BF16)
    for n, a in enumerate(MSG_RIGHT):
        m_rt[n] = rows(a, 0, CJ - 1, 16).astype(BF16)
    for m, (di, dj, fields) in enumerate(CORNERS):
        for n, a in enumerate(fields):
            at = a * AREA + (2 + (0 if di < 0 else RI - 1)) * XC + 8 + (0 if dj < 0 else CJ - 1)
            m_co[m, n : n + 1] = ld(xf, at, 1)

    pl.semaphore_wait(barrier, len(partners))

    def remote(src, dst, ssem, rsem, to):
        return pltpu.make_async_remote_copy(
            src_ref=src, dst_ref=dst, send_sem=ssem, recv_sem=rsem, device_id=to, device_id_type=MESH
        )

    halo = [
        remote(m_up, r_bot, hs.at[0], hr.at[0], near(-1, 0)),
        remote(m_dn, r_top, hs.at[1], hr.at[1], near(1, 0)),
        remote(m_lf, r_rt, hs.at[2], hr.at[2], near(0, -1)),
        remote(m_rt, r_lf, hs.at[3], hr.at[3], near(0, 1)),
    ]
    for m, (di, dj, _) in enumerate(CORNERS):
        halo.append(remote(m_co.at[m], r_co.at[m], hs.at[4 + m], hr.at[4 + m], near(di, dj)))
    for c in halo:
        c.start()

    for c in loads[3:]:
        c.wait()

    def turn(t, carry):
        at = pl.multiple_of(t * CH, CH)
        convwt[pl.ds(at, CH), :] = convw[pl.ds(at, CH), :].T
        upwt[pl.ds(at, CH), :] = upw[pl.ds(at, CH), :].T
        return carry

    lax.fori_loop(0, 9, turn, 0)
    src = lax.broadcasted_iota(jnp.int32, (CH, CH), 0)
    dst = lax.broadcasted_iota(jnp.int32, (CH, CH), 1)
    wanted = (((dst % HL) // CB) * XL + dst // HL) * CB + dst % CB
    perm = jnp.where(src == wanted, 1.0, 0.0).astype(BF16)

    for c in halo:
        c.wait()
    keep_top = jnp.where(band == 0, 0.0, 1.0)
    keep_bot = jnp.where(band == nband - 1, 0.0, 1.0)
    for n, a in enumerate(MSG_UP):
        st(xf, a * AREA + (RI + 2) * XC + 8, CJ, r_bot[n].astype(F32) * keep_bot)
    for n, a in enumerate(MSG_DOWN):
        st(xf, a * AREA + XC + 8, CJ, r_top[n].astype(F32) * keep_top)
    for n, a in enumerate(MSG_LEFT):
        st(xf, a * AREA + 2 * XC + 8 + CJ, RI, r_rt[n].astype(F32)[:RI], XC)
    for n, a in enumerate(MSG_RIGHT):
        st(xf, a * AREA + 2 * XC + 7, RI, r_lf[n].astype(F32)[:RI], XC)
    for m, (di, dj, fields) in enumerate(CORNERS):
        keep = keep_bot if di < 0 else keep_top
        for n, a in enumerate(fields):
            at = a * AREA + (RI + 2 if di < 0 else 1) * XC + (8 + CJ if dj < 0 else 7)
            st(xf, at, 1, r_co[m, n : n + 1] * keep)

    def window(ref, a, i, dj, n):
        return jnp.concatenate(
            [ld(ref, a * AREA + (i + q + 2) * XC + 8 + dj, CJ) for q in range(n)], axis=0
        )

    for di in range(2):
        for dj in range(2):
            ce[2 * di + dj, :224] = window(xf, 0, di - 1, dj, 14).astype(BF16)
            ce[2 * di + dj, 224:240] = rows(0, di - 1, dj - 1, 16).astype(BF16)
            ce[2 * di + dj, 240:] = rows(0, di - 1, CJ, 16).astype(BF16)
    line = lax.broadcasted_iota(jnp.int32, (CH, CH), 0)
    cell_row = jnp.where(line < 224, line // 16, line % 16)
    ghost = ((band == 0) & (cell_row == 0)) | ((band == nband - 1) & (cell_row == 13))
    for r in range(2):
        for s in range(2):
            ph = 2 * r + s
            total = None
            for k, di in ((1, 0),) if r == 0 else ((2, 0), (0, 1)):
                for l, dj in ((1, 0),) if s == 0 else ((2, 0), (0, 1)):
                    term = dot(ce[2 * di + dj], upw[(3 * k + l) * CH : (3 * k + l + 1) * CH, :])
                    total = term if total is None else total + term
            skip_e = jnp.concatenate(
                [window(xf, 1 + ph, -1, 0, 14), rows(1 + ph, -1, -1, 16), rows(1 + ph, -1, CJ, 16)], axis=0
            )
            pre = total + skip_e
            sig = jax.nn.sigmoid(pre)
            act = jnp.where(ghost, 0.0, pre * sig).astype(BF16).astype(F32)
            dfac[ph] = jnp.where(ghost, 0.0, sig * (1.0 + pre * (1.0 - sig)))
            for q in range(14):
                st(af, ph * AREA + (q + 1) * XC + 8, CJ, act[16 * q : 16 * q + 16])
            st(af, ph * AREA + XC + 7, 16, act[224:240], XC)
            st(af, ph * AREA + XC + 8 + CJ, 16, act[240:], XC)
            actt[:, ph * 192 : ph * 192 + 192] = act[16:208].T.astype(BF16)

    for r in range(2):
        for s in range(2):
            for v, dj in enumerate((0, 1 if s == 0 else -1)):
                n = (2 * r + s) * 2 + v
                tv[n] = window(xf, 5 + 2 * r + s, -1, dj, 14).astype(BF16)
                tvp[n] = dot(tv[n], perm).astype(BF16)

    def view(ref, er, es, i0, n):
        (r, di), (s, dj) = split(er), split(es)
        at = (i0 + di + 1) * 16
        return ref[(2 * r + s) * 2 + (1 if dj else 0), at : at + 16 * n]

    def put(arr, t, value):
        start = t * CH
        while start < (t + 1) * CH:
            f, off = divmod(start, FB)
            stop = min((t + 1) * CH, (f + 1) * FB)
            gsum[arr, f // (2 * Y), (f // 2) % Y, f % 2, off : off + stop - start] = value[
                start - t * CH : stop - t * CH
            ]
            start = stop

    for t, (k, l) in enumerate(TAPS):
        right = jnp.concatenate(
            [view(tvp, r - k + 1, s - l + 1, 0, RI) for r in range(2) for s in range(2)], axis=0
        )
        put(0, t, dot(actt[...], right).astype(BF16))

    def first(arr):
        return remote(
            gsum.at[arr, :, :, 1 - core], r0.at[arr], s0s.at[arr], s0r.at[arr], at_core()
        )

    def second(arr):
        def add(n, carry):
            a, b = n // Y, n % Y
            total = gsum[arr, a, b, core].astype(F32) + r0[arr, a, b].astype(F32)
            s1[arr, a, b] = total.astype(BF16)
            return carry

        lax.fori_loop(0, XH * Y, add, 0)

    step0c = first(0)
    step0c.start()

    for r in range(2):
        for s in range(2):
            ph = 2 * r + s
            i0 = -1 if r else 0
            n = RI - i0
            left = jnp.concatenate([view(tv, r - k + 1, s - l + 1, i0, n) for k, l in TAPS], axis=1)
            if s:
                column = []
                for k, l in TAPS:
                    (r2, di), (s2, dj) = split(r - k + 1), split(s - l + 1)
                    column.append(rows(5 + 2 * r2 + s2, -1 + di, -1 + dj, 16).astype(BF16))
                left = jnp.concatenate([left, jnp.concatenate(column, axis=1)], axis=0)
            grad = dot(left, convwt[...])
            main = (grad[: 16 * n] * dfac[ph, (i0 + 1) * 16 : 208]).astype(BF16).astype(F32)
            for q in range(n):
                st(gf, ph * AREA + (i0 + q + 2) * XC + 8, CJ, main[16 * q : 16 * q + 16])
            if s:
                side = (grad[16 * n :] * dfac[ph, 224:240]).astype(BF16).astype(F32)
                st(gf, ph * AREA + XC + 7, 16, side, XC)

    step0c.wait()
    second(0)
    step1c = [
        remote(s1.at[0, :, (yy + d) % Y], r1c.at[Y - d - 1], s1s.at[0, d - 1], s1r.at[0, Y - d - 1], at_y(d))
        for d in range(1, Y)
    ]
    for c in step1c:
        c.start()

    coarse_t = window(xf, 0, 0, 0, RI).T.astype(BF16)
    for t, (k, l) in enumerate(TAPS):
        (r, di), (s, dj) = split(k - 1), split(l - 1)
        part = window(gf, 2 * r + s, di, dj, RI).astype(BF16)
        gv[:, t * CH : (t + 1) * CH] = part
        put(1, t, dot(coarse_t, dot(part, perm).astype(BF16)).astype(BF16))

    step0u = first(1)
    step0u.start()

    for r in range(2):
        for s in range(2):
            for v, dj in enumerate((0, 1 if s == 0 else -1)):
                av[(2 * r + s) * 2 + v] = window(af, 2 * r + s, -1, dj, 14).astype(BF16)

    step0u.wait()
    second(1)

    def x_piece(ref, d):
        x2 = (xx + d) % NX
        return ref.at[x2 // XL, :, :, pl.ds(pl.multiple_of((x2 % XL) * HL, HL), HL)]

    step1u = [
        remote(x_piece(s1.at[1], d), r1u.at[NX - d - 1], s1s.at[1, d - 1], s1r.at[1, NX - d - 1], at_x(d))
        for d in range(1, NX)
    ]
    for c in step1u:
        c.start()

    def decode(r, s):
        left = jnp.concatenate([view(av, r + k - 1, s + l - 1, 0, RI) for k, l in TAPS], axis=1)
        out = dot(left, convw[...])
        for i in range(RI):
            st(dec_v, (2 * i + r) * 2 * CJ + s, CJ, out[16 * i : 16 * i + 16], 2)

    decode(0, 0)
    decode(0, 1)

    for c in step1c:
        c.wait()
    for a in range(XH):
        total = gsum[0, a, yy, core].astype(F32) + r0[0, a, yy].astype(F32)
        for d in range(Y - 1):
            total = total + r1c[d, a].astype(F32)
        a1c[a] = total
        s2c[a] = total.astype(BF16)

    def x_piece2(ref, d):
        x2 = (xx + d) % NX
        return ref.at[x2 // XL, :, pl.ds(pl.multiple_of((x2 % XL) * HL, HL), HL)]

    step2c = [
        remote(x_piece2(s2c, d), r2c.at[NX - d - 1], s2s.at[0, d - 1], s2r.at[0, NX - d - 1], at_x(d))
        for d in range(1, NX)
    ]
    for c in step2c:
        c.start()

    decode(1, 0)
    decode(1, 1)

    own = pl.ds(pl.multiple_of(xl * HL, HL), HL)
    for c in step1u:
        c.wait()
    for b in range(Y):
        total = gsum[1, xh, b, core, :, own].astype(F32) + r0[1, xh, b, :, own].astype(F32)
        for d in range(NX - 1):
            total = total + r1u[d, b].astype(F32)
        a1u[b] = total
        s2u[b] = total.astype(BF16)
    step2u = [
        remote(s2u.at[(yy + d) % Y], r2u.at[Y - d - 1], s2s.at[1, d - 1], s2r.at[1, Y - d - 1], at_y(d))
        for d in range(1, Y)
    ]
    for c in step2u:
        c.start()

    def third(arr, total):
        pad[arr, :FB] = total
        turned = pad[arr].T
        for z in range(Z):
            a3[arr, z] = turned[z * CB : (z + 1) * CB]
            s3[arr, z] = turned[z * CB : (z + 1) * CB].astype(BF16)
        steps = [
            remote(s3.at[arr, (zz + d) % Z], r3.at[arr, Z - d - 1], s3s.at[arr, d - 1], s3r.at[arr, Z - d - 1], at_z(d))
            for d in range(1, Z)
        ]
        for c in steps:
            c.start()
        return steps

    for c in step2c:
        c.wait()
    total = a1c[xh, :, own]
    for d in range(NX - 1):
        total = total + r2c[d].astype(F32)
    step3c = third(0, total)

    gc_v[...] = dot(gv[...], upwt[...]).astype(BF16)
    gc_copy = pltpu.make_async_copy(gc_v, gc_h, out_sem.at[0])
    gc_copy.start()
    for p in range(2 * RI):
        skip_v[p] = ld(dec_v, p * 2 * CJ, 2 * CJ).astype(BF16)
    dec_copy = pltpu.make_async_copy(skip_v, dec_h, out_sem.at[1])
    dec_copy.start()

    for c in step2u:
        c.wait()
    total = a1u[yy]
    for d in range(Y - 1):
        total = total + r2u[d].astype(F32)
    step3u = third(1, total)

    for arr, steps, out in ((0, step3c, gw_o), (1, step3u, gu_o)):
        for c in steps:
            c.wait()
        total = a3[arr, zz]
        for d in range(Z - 1):
            total = total + r3[arr, d].astype(F32)
        out[...] = total
    gc_copy.wait()
    dec_copy.wait()


def local(dims, coarse, skip, up_weight, conv_weight, cotangent):
    XH, Y, Z, XL = dims
    NX, HL = XH * XL, CH // XL
    FB, CB = 9 * CH // (XH * Y * 2), CH // (Z * XL)
    FP = -(-FB // 128) * 128
    any_, vmem = pl.BlockSpec(memory_space=pl.ANY), pl.BlockSpec(memory_space=pltpu.VMEM)
    V, dma = pltpu.VMEM, pltpu.SemaphoreType.DMA
    scratch = [
        V((RI, CJ, CH), BF16), V((2 * RI, 2 * CJ, CH), BF16), V((2 * RI, 2 * CJ, CH), BF16),
        V((9 * CH, CH), BF16), V((9 * CH, CH), BF16), V((9 * CH, CH), BF16), V((9 * CH, CH), BF16),
        V((2, 9 * AREA, 128), F32), V((2, 4 * CJ, 128), F32), V((2, 4 * CJ, 128), F32),
        V((2, 4 * AREA, 128), F32), V((2, 4 * AREA, 128), F32), V((4, CH, CH), F32),
        V((4, CH, CH), BF16), V((8, 224, CH), BF16), V((8, 224, CH), BF16), V((8, 224, CH), BF16),
        V((192, 9 * CH), BF16), V((CH, 768), BF16), V((2, 4 * RI * CJ, 128), F32), V((192, CH), BF16),
        V((5, 16, CH), BF16), V((7, 16, CH), BF16), V((5, 16, CH), BF16), V((7, 16, CH), BF16), V((4, 8, CH), F32),
        V((5, 16, CH), BF16), V((7, 16, CH), BF16), V((5, 16, CH), BF16), V((7, 16, CH), BF16), V((4, 8, CH), F32),
        V((2, XH, Y, 2, FB, CH), BF16), V((2, XH, Y, FB, CH), BF16), V((2, XH, Y, FB, CH), BF16),
        V((Y - 1, XH, FB, CH), BF16), V((NX - 1, Y, FB, HL), BF16),
        V((XH, FB, CH), F32), V((Y, FB, HL), F32), V((XH, FB, CH), BF16), V((Y, FB, HL), BF16),
        V((NX - 1, FB, HL), BF16), V((Y - 1, FB, HL), BF16),
        V((2, FP, HL), F32), V((2, Z, CB, FP), F32), V((2, Z, CB, FP), BF16), V((2, Z - 1, CB, FP), BF16),
        dma((5,)), dma((2,)), dma((8,)), dma((8,)), dma((2,)), dma((2,)),
        dma((2, 3)), dma((2, 3)), dma((2, 3)), dma((2, 3)), dma((2, Z - 1)), dma((2, Z - 1)),
    ]
    decoded, grad_coarse, grad_up, grad_conv = pl.pallas_call(
        functools.partial(kernel, dims),
        out_shape=(
            jax.ShapeDtypeStruct((2 * RI, 2 * CJ, CH), BF16),
            jax.ShapeDtypeStruct((RI * CJ, CH), BF16),
            jax.ShapeDtypeStruct((CB, FP), F32),
            jax.ShapeDtypeStruct((CB, FP), F32),
        ),
        in_specs=[any_] * 5,
        out_specs=(any_, any_, vmem, vmem),
        scratch_shapes=scratch,
        compiler_params=pltpu.CompilerParams(
            collective_id=0, has_side_effects=True, vmem_limit_bytes=60 * 2**20
        ),
    )(coarse, skip, up_weight.reshape(9 * CH, CH), conv_weight.reshape(9 * CH, CH), cotangent)
    return (
        decoded,
        grad_coarse.reshape(RI, CJ, CH),
        grad_up[:, :FB].T,
        grad_conv[:, :FB].T,
    )


def build(mesh, dims):
    cells = P("band", "face", None)
    return jax.shard_map(
        functools.partial(local, dims),
        mesh=mesh,
        in_specs=(cells, cells, P(), P(), cells),
        out_specs=(cells, cells, P("face", "band"), P("face", "band")),
        check_vma=False,
    )


def solution(mesh):
    return build(mesh, (2, 4, 8, 2))
```

time: 386 us -> 47.2 us (0.12)
  the two profiles are of different devices: /device:TPU:8 before, /device:TPU:1 now
where the time goes in v1:
time: 47.2 us; the launch traced here: 46.8 us
  Pallas kernels  41.6 us (88%)
  local copies, waits for them, and re-layouts  4.65 us (10%)
  between operations  0.64 us (1%)
    pallas_call x1, Pallas kernels, local(): pl.pallas_call(functools.partial(kernel, dims), out_shape=(jax.ShapeDtype...  41.6 us
    unnamed x2, local copies, waits for them, and re-layouts  3.3 us
    transpose x1, local copies, waits for them, and re-layouts, local(): grad_conv[:, :FB]  1.35 us

profile of v1, /device:TPU:1, one launch (start us, length us, event | category | flops | bytes accessed | tf_op | source)
XLA Modules:
  0.0 46.8 jit_solution(6749628658288252149)
XLA Ops:
  0.6 41.6 %shard_map.84 = (bf16[24,32,256]{2,1,0:T(8,128)(2,1)}, bf16[192,256]{1,0:T(8,128)(2,1)}, f32[16,256]{1,0:T(8,128)}, f32[16,256]{1,0:T(8,128)}) custom-call(bf16[12,16,256]{2,1,0:T(8,128)(2,1)} %coarse_h.1, bf16[24,32,256]{2,1,0:T(8,128)(2,1)} %skip_h.1, bf16[2304,256]{1,0:T(8,128)(2,1)} %bitcast.7, bf16[2304,256]{1,0:T(8,128)(2,1)} %bitcast.8, ...), custom_call_target="tpu_custom_call" | custom-call | tf_op jit(solution)/shard_map/pallas_call | solution.py:455
  42.2 1.3 %slice_bitcast_fusion = (f32[144,16]{0,1:T(8,128)}, f32[144,16]{0,1:T(8,128)}) fusion(f32[16,256]{1,0:T(8,128)} %get-tuple-element.11, f32[16,256]{1,0:T(8,128)} %get-tuple-element.10), kind=kLoop, calls=%fused_computation | loop fusion | bytes 36864 | tf_op jit(solution)/shard_map/transpose | solution.py:474
  43.5 1.8 %copy.11 = bf16[24,32,256]{2,1,0:T(8,128)(2,1)} copy(bf16[24,32,256]{2,1,0:T(8,128)(2,1)} %get-tuple-element.18) | data formatting | bytes 786432
  45.3 1.5 %copy.12 = bf16[12,16,256]{2,1,0:T(8,128)(2,1)} copy(bf16[12,16,256]{2,1,0:T(8,128)(2,1)} %bitcast.9) | data formatting | bytes 196608

commit v2 on v1

v2 whole, which is shorter than its diff:
```python
import functools

import jax
import jax.numpy as jnp
from jax import lax
from jax.experimental import pallas as pl
from jax.experimental.pallas import tpu as pltpu
from jax.sharding import PartitionSpec as P

F32, BF16 = jnp.float32, jnp.bfloat16
MESH = pl.DeviceIdType.MESH
CH = 256
RI, CJ = 12, 16
XR, XC = 18, 32
AREA = XR * XC

UP1, UP2 = (0, 5, 6), (1, 2)
DOWN1, DOWN2 = (7, 8), (0, 3, 4, 5, 6)
LEFT1, LEFT2 = (0, 5, 7), (1, 3)
RIGHT1, RIGHT2 = (6, 8), (0, 2, 4, 5, 7)
CORNERS = (
    (-1, -1, (0, 1, 5)),
    (-1, 1, (0, 2, 5, 6)),
    (1, -1, (0, 3, 5, 7)),
    (1, 1, (0, 4, 5, 6, 7, 8)),
)
TAPS = [(k, l) for k in range(3) for l in range(3)]


def split(e):
    return e % 2, e // 2


def dot(a, b):
    return jnp.dot(a, b, preferred_element_type=F32)


def ld(ref, at, n, stride=1):
    if stride == 1:
        return jnp.concatenate([ref[h, pl.ds(at, n), :] for h in range(2)], axis=-1)
    return jnp.concatenate([ref[h, pl.ds(at, n, stride=stride), :] for h in range(2)], axis=-1)


def st(ref, at, n, value, stride=1):
    for h in range(2):
        part = value[:, 128 * h : 128 * h + 128]
        if stride == 1:
            ref[h, pl.ds(at, n), :] = part
        else:
            ref[h, pl.ds(at, n, stride=stride), :] = part


def kernel(
    dims,
    coarse_h, skip_h, upw_h, convw_h, cot_h,
    dec_o, gc_o, gu_o, gw_o,
    coarse_v, skip_v, cot_v, upw, convw, upwt, convwt,
    xf, fs, ft, af, gf, dfac, dghost, ce, cg, tv, tvp, av, gv, actt, dec_v,
    m_1, m_2, m_co, r_1, r_2, r_co,
    gsum, r0, s1, r1a, r1b, a1a, a1b, s2a, s2b, r2a, r2b, pad, a3, s3, r3,
    in_sem, hs, hr, s0s, s0r, s1s, s1r, s2s, s2r, s3s, s3r,
):
    loads = [
        pltpu.make_async_copy(src, dst, in_sem.at[n])
        for n, (src, dst) in enumerate(
            ((coarse_h, coarse_v), (cot_h, cot_v), (skip_h, skip_v), (convw_h, convw), (upw_h, upw))
        )
    ]
    for c in loads:
        c.start()

    XH, Y, Z, XL = dims
    NX = XH * XL
    HL = CH // XL
    FB = 9 * CH // (XH * Y * 2)
    RA = FB // 16 * 5 // 9 * 16
    CB = CH // (Z * XL)
    nface, nband = XH * Y * 2, Z * XL
    face, band = lax.axis_index("face"), lax.axis_index("band")
    core = face % 2
    yy = (face // 2) % Y
    xh = face // (2 * Y)
    xl = band % XL
    zz = band // XL
    xx = xh * XL + xl

    def dev(xx_, yy_, core_, zz_):
        return {
            "face": (xx_ // XL) * (2 * Y) + yy_ * 2 + core_,
            "band": zz_ * XL + xx_ % XL,
        }

    def near(di, dj):
        return {"face": (face + dj + nface) % nface, "band": (band + di + nband) % nband}

    def at_core():
        return dev(xx, yy, 1 - core, zz)

    def at_y(d):
        return dev(xx, (yy + d) % Y, core, zz)

    def at_x(d):
        return dev((xx + d) % NX, yy, core, zz)

    def at_z(d):
        return dev(xx, yy, core, (zz + d) % Z)

    ways = [(-1, 0), (1, 0), (0, -1), (0, 1), (-1, -1), (-1, 1), (1, -1), (1, 1)]
    partners = [near(*w) for w in ways] + [at_core()]
    partners += [at_y(d) for d in range(1, Y)] + [at_x(d) for d in range(1, NX)]
    partners += [at_z(d) for d in range(1, Z)]
    barrier = pltpu.get_barrier_semaphore()
    for p in partners:
        pl.semaphore_signal(barrier, inc=1, device_id=p, device_id_type=MESH)

    def rows(a, i, col, n):
        return ld(xf, a * AREA + (i + 2) * XC + 8 + col, n, XC)

    for c in loads[:3]:
        c.wait()

    def spread(i, carry):
        base = pl.multiple_of((i + 2) * XC + 8, 8)
        st(xf, base, CJ, coarse_v[i].astype(F32))
        for src, stage, first in ((skip_v, fs, 1), (cot_v, ft, 5)):
            for r in range(2):
                st(stage, r * 2 * CJ, 2 * CJ, src[2 * i + r].astype(F32))
            for r in range(2):
                for s in range(2):
                    part = ld(stage, r * 2 * CJ + s, CJ, 2)
                    st(xf, pl.multiple_of(base + (first + 2 * r + s) * AREA, 8), CJ, part)
        return carry

    lax.fori_loop(0, RI, spread, 0)

    def message(buf, fields, way):
        for n, a in enumerate(fields):
            if way < 2:
                buf[way, n] = ld(xf, a * AREA + (2 if way == 0 else RI + 1) * XC + 8, CJ).astype(BF16)
            else:
                buf[way, n] = rows(a, 0, 0 if way == 2 else CJ - 1, 16).astype(BF16)

    for way, fields in enumerate((UP1, DOWN1, LEFT1, RIGHT1)):
        message(m_1, fields, way)
    for m, (di, dj, fields) in enumerate(CORNERS):
        for n, a in enumerate(fields):
            at = a * AREA + (2 + (0 if di < 0 else RI - 1)) * XC + 8 + (0 if dj < 0 else CJ - 1)
            m_co[m, n : n + 1] = ld(xf, at, 1)

    pl.semaphore_wait(barrier, len(partners))

    def remote(src, dst, ssem, rsem, to):
        return pltpu.make_async_remote_copy(
            src_ref=src, dst_ref=dst, send_sem=ssem, recv_sem=rsem, device_id=to, device_id_type=MESH
        )

    halo1, halo2 = [], []
    for m, (di, dj, _) in enumerate(CORNERS):
        halo1.append(remote(m_co.at[m], r_co.at[m], hs.at[m], hr.at[m], near(di, dj)))
    for way, fields in enumerate((UP1, DOWN1, LEFT1, RIGHT1)):
        n = len(fields)
        halo1.append(
            remote(m_1.at[way, :n], r_1.at[way, :n], hs.at[4 + way], hr.at[4 + way], near(*ways[way]))
        )
    for c in halo1:
        c.start()
    for way, fields in enumerate((UP2, DOWN2, LEFT2, RIGHT2)):
        message(m_2, fields, way)
        n = len(fields)
        halo2.append(
            remote(m_2.at[way, :n], r_2.at[way, :n], hs.at[8 + way], hr.at[8 + way], near(*ways[way]))
        )
    for c in halo2:
        c.start()

    for c in loads[3:]:
        c.wait()

    def turn(t, carry):
        at = pl.multiple_of(t * CH, CH)
        convwt[pl.ds(at, CH), :] = convw[pl.ds(at, CH), :].T
        upwt[pl.ds(at, CH), :] = upw[pl.ds(at, CH), :].T
        return carry

    lax.fori_loop(0, 9, turn, 0)
    src = lax.broadcasted_iota(jnp.int32, (CH, CH), 0)
    dst = lax.broadcasted_iota(jnp.int32, (CH, CH), 1)
    wanted = (((dst % HL) // CB) * XL + dst // HL) * CB + dst % CB
    perm = jnp.where(src == wanted, 1.0, 0.0).astype(BF16)

    keep_top = jnp.where(band == 0, 0.0, 1.0)
    keep_bot = jnp.where(band == nband - 1, 0.0, 1.0)

    def receive(buf, fields, way):
        for n, a in enumerate(fields):
            value = buf[way, n].astype(F32)
            if way == 0:
                st(xf, a * AREA + (RI + 2) * XC + 8, CJ, value * keep_bot)
            elif way == 1:
                st(xf, a * AREA + XC + 8, CJ, value * keep_top)
            else:
                st(xf, a * AREA + 2 * XC + (8 + CJ if way == 2 else 7), RI, value[:RI], XC)

    for c in halo1:
        c.wait()
    for way, fields in enumerate((UP1, DOWN1, LEFT1, RIGHT1)):
        receive(r_1, fields, way)
    for m, (di, dj, fields) in enumerate(CORNERS):
        keep = keep_bot if di < 0 else keep_top
        for n, a in enumerate(fields):
            at = a * AREA + (RI + 2 if di < 0 else 1) * XC + (8 + CJ if dj < 0 else 7)
            st(xf, at, 1, r_co[m, n : n + 1] * keep)

    def window(ref, a, i, dj, n):
        return jnp.concatenate(
            [ld(ref, a * AREA + (i + q + 2) * XC + 8 + dj, CJ) for q in range(n)], axis=0
        )

    def up(left, r, s):
        total = None
        for k, di in ((1, 0),) if r == 0 else ((2, 0), (0, 1)):
            for l, dj in ((1, 0),) if s == 0 else ((2, 0), (0, 1)):
                term = dot(left[2 * di + dj], upw[(3 * k + l) * CH : (3 * k + l + 1) * CH, :])
                total = term if total is None else total + term
        return total

    for di in range(2):
        for dj in range(2):
            ce[2 * di + dj] = window(xf, 0, di, dj, RI).astype(BF16)
    for r in range(2):
        for s in range(2):
            ph = 2 * r + s
            pre = up(ce, r, s) + window(xf, 1 + ph, 0, 0, RI)
            sig = jax.nn.sigmoid(pre)
            act = (pre * sig).astype(BF16).astype(F32)
            dfac[ph] = sig * (1.0 + pre * (1.0 - sig))
            for q in range(RI):
                st(af, ph * AREA + (q + 2) * XC + 8, CJ, act[16 * q : 16 * q + 16])
            actt[:, ph * 192 : ph * 192 + 192] = act.T.astype(BF16)

    for r in range(2):
        for s in range(2):
            for v, dj in enumerate((0, 1 if s == 0 else -1)):
                n = (2 * r + s) * 2 + v
                tv[n] = window(xf, 5 + 2 * r + s, -1, dj, 14).astype(BF16)
                tvp[n] = dot(tv[n], perm).astype(BF16)

    def view(ref, er, es, i0, n):
        (r, di), (s, dj) = split(er), split(es)
        at = (i0 + di + 1) * 16
        return ref[(2 * r + s) * 2 + (1 if dj else 0), at : at + 16 * n]

    def put(arr, t, value):
        start = t * CH
        while start < (t + 1) * CH:
            f, off = divmod(start, FB)
            stop = min((t + 1) * CH, (f + 1) * FB)
            gsum[arr, f // (2 * Y), (f // 2) % Y, f % 2, off : off + stop - start] = value[
                start - t * CH : stop - t * CH
            ]
            start = stop

    for t, (k, l) in enumerate(TAPS):
        right = jnp.concatenate(
            [view(tvp, r - k + 1, s - l + 1, 0, RI) for r in range(2) for s in range(2)], axis=0
        )
        put(0, t, dot(actt[...], right).astype(BF16))

    def first(arr):
        return remote(
            gsum.at[arr, :, :, 1 - core], r0.at[arr], s0s.at[arr], s0r.at[arr], at_core()
        )

    def second(arr):
        def add(n, carry):
            a, b = n // Y, n % Y
            total = gsum[arr, a, b, core].astype(F32) + r0[arr, a, b].astype(F32)
            s1[arr, a, b] = total.astype(BF16)
            return carry

        lax.fori_loop(0, XH * Y, add, 0)

    step0c = first(0)
    step0c.start()

    for c in halo2:
        c.wait()
    for way, fields in enumerate((UP2, DOWN2, LEFT2, RIGHT2)):
        receive(r_2, fields, way)

    def border(a, di, dj):
        return jnp.concatenate(
            [window(xf, a, di - 1, dj, 1), window(xf, a, di + RI, dj, 1)]
            + [rows(a, di - 1, dj - 1, 16), rows(a, di - 1, dj + CJ, 16)],
            axis=0,
        )

    for di in range(2):
        for dj in range(2):
            cg[2 * di + dj] = border(0, di, dj).astype(BF16)
    line = lax.broadcasted_iota(jnp.int32, (64, CH), 0)
    first_row = (line < 16) | ((line >= 32) & (line % 16 == 0))
    last_row = ((line >= 16) & (line < 32)) | ((line >= 32) & (line % 16 == RI + 1))
    ghost = ((band == 0) & first_row) | ((band == nband - 1) & last_row)
    for r in range(2):
        for s in range(2):
            ph = 2 * r + s
            pre = up(cg, r, s) + border(1 + ph, 0, 0)
            sig = jax.nn.sigmoid(pre)
            act = jnp.where(ghost, 0.0, pre * sig).astype(BF16).astype(F32)
            dghost[ph] = jnp.where(ghost, 0.0, sig * (1.0 + pre * (1.0 - sig)))
            st(af, ph * AREA + XC + 8, CJ, act[:16])
            st(af, ph * AREA + (RI + 2) * XC + 8, CJ, act[16:32])
            st(af, ph * AREA + XC + 7, 16, act[32:48], XC)
            st(af, ph * AREA + XC + 8 + CJ, 16, act[48:], XC)

    for s in range(2):
        for v, dj in enumerate((0, 1 if s == 0 else -1)):
            tv[2 * s + v, :16] = window(xf, 5 + s, -1, dj, 1).astype(BF16)

    for r in range(2):
        for s in range(2):
            ph = 2 * r + s
            i0 = -1 if r else 0
            n = RI - i0
            left = jnp.concatenate([view(tv, r - k + 1, s - l + 1, i0, n) for k, l in TAPS], axis=1)
            if s:
                column = []
                for k, l in TAPS:
                    (r2, di), (s2, dj) = split(r - k + 1), split(s - l + 1)
                    column.append(rows(5 + 2 * r2 + s2, -1 + di, -1 + dj, 16).astype(BF16))
                left = jnp.concatenate([left, jnp.concatenate(column, axis=1)], axis=0)
            grad = dot(left, convwt[...])
            slope = jnp.concatenate([dghost[ph, :16], dfac[ph]], axis=0) if r else dfac[ph]
            main = (grad[: 16 * n] * slope).astype(BF16).astype(F32)
            for q in range(n):
                st(gf, ph * AREA + (i0 + q + 2) * XC + 8, CJ, main[16 * q : 16 * q + 16])
            if s:
                side = (grad[16 * n :] * dghost[ph, 32:48]).astype(BF16).astype(F32)
                st(gf, ph * AREA + XC + 7, 16, side, XC)

    coarse_t = window(xf, 0, 0, 0, RI).T.astype(BF16)
    for t, (k, l) in enumerate(TAPS):
        (r, di), (s, dj) = split(k - 1), split(l - 1)
        part = window(gf, 2 * r + s, di, dj, RI).astype(BF16)
        gv[:, t * CH : (t + 1) * CH] = part
        put(1, t, dot(coarse_t, dot(part, perm).astype(BF16)).astype(BF16))
    step0u = first(1)
    step0u.start()

    def half(x2):
        return pl.ds(pl.multiple_of((x2 % XL) * HL, HL), HL)

    def stage1(arr):
        steps = [[], []]
        for d in range(1, max(Y, NX)):
            if d < Y:
                q = Y - d - 1
                steps[0].append(
                    remote(
                        s1.at[arr, :, (yy + d) % Y, :RA], r1a.at[arr, q],
                        s1s.at[arr, 0, d - 1], s1r.at[arr, 0, q], at_y(d),
                    )
                )
                steps[0][-1].start()
            if d < NX:
                q, x2 = NX - d - 1, (xx + d) % NX
                steps[1].append(
                    remote(
                        s1.at[arr, x2 // XL, :, RA:, half(x2)], r1b.at[arr, q],
                        s1s.at[arr, 1, d - 1], s1r.at[arr, 1, q], at_x(d),
                    )
                )
                steps[1][-1].start()
        return steps

    def stage2a(arr, steps):
        for c in steps:
            c.wait()
        for a in range(XH):
            total = gsum[arr, a, yy, core, :RA].astype(F32) + r0[arr, a, yy, :RA].astype(F32)
            for d in range(Y - 1):
                total = total + r1a[arr, d, a].astype(F32)
            a1a[arr, a] = total
            s2a[arr, a] = total.astype(BF16)
        out = []
        for d in range(1, NX):
            q, x2 = NX - d - 1, (xx + d) % NX
            out.append(
                remote(
                    s2a.at[arr, x2 // XL, :, half(x2)], r2a.at[arr, q],
                    s2s.at[arr, 0, d - 1], s2r.at[arr, 0, q], at_x(d),
                )
            )
            out[-1].start()
        return out

    def stage2b(arr, steps):
        for c in steps:
            c.wait()
        own = half(xx)
        for b in range(Y):
            total = gsum[arr, xh, b, core, RA:, own].astype(F32) + r0[arr, xh, b, RA:, own].astype(F32)
            for d in range(NX - 1):
                total = total + r1b[arr, d, b].astype(F32)
            a1b[arr, b] = total
            s2b[arr, b] = total.astype(BF16)
        out = []
        for d in range(1, Y):
            q = Y - d - 1
            out.append(
                remote(
                    s2b.at[arr, (yy + d) % Y], r2b.at[arr, q],
                    s2s.at[arr, 1, d - 1], s2r.at[arr, 1, q], at_y(d),
                )
            )
            out[-1].start()
        return out

    def stage3(arr, steps):
        for c in steps[0]:
            c.wait()
        total = a1a[arr, xh, :, half(xx)]
        for d in range(NX - 1):
            total = total + r2a[arr, d].astype(F32)
        pad[arr, :RA] = total
        for c in steps[1]:
            c.wait()
        total = a1b[arr, yy]
        for d in range(Y - 1):
            total = total + r2b[arr, d].astype(F32)
        pad[arr, RA:FB] = total
        turned = pad[arr].T
        for z in range(Z):
            a3[arr, z] = turned[z * CB : (z + 1) * CB]
            s3[arr, z] = turned[z * CB : (z + 1) * CB].astype(BF16)
        out = []
        for d in range(1, Z):
            q = Z - d - 1
            out.append(
                remote(s3.at[arr, (zz + d) % Z], r3.at[arr, q], s3s.at[arr, d - 1], s3r.at[arr, q], at_z(d))
            )
            out[-1].start()
        return out

    def finish(arr, steps, out):
        for c in steps:
            c.wait()
        total = a3[arr, zz]
        for d in range(Z - 1):
            total = total + r3[arr, d].astype(F32)
        out[...] = total[:, :FB]

    def decode(r, s):
        left = jnp.concatenate([view(av, r + k - 1, s + l - 1, 0, RI) for k, l in TAPS], axis=1)
        out = dot(left, convw[...])
        for i in range(RI):
            st(dec_v, (2 * i + r) * 2 * CJ + s, CJ, out[16 * i : 16 * i + 16], 2)

    step0c.wait()
    second(0)
    step1c = stage1(0)

    for r in range(2):
        for s in range(2):
            for v, dj in enumerate((0, 1 if s == 0 else -1)):
                av[(2 * r + s) * 2 + v] = window(af, 2 * r + s, -1, dj, 14).astype(BF16)

    step0u.wait()
    second(1)
    step1u = stage1(1)

    decode(0, 0)
    decode(0, 1)
    step2c = [stage2a(0, step1c[0]), stage2b(0, step1c[1])]
    decode(1, 0)
    decode(1, 1)
    step3c = stage3(0, step2c)
    gc_o[...] = dot(gv[...], upwt[...]).astype(BF16)
    for p in range(2 * RI):
        dec_o[p] = ld(dec_v, p * 2 * CJ, 2 * CJ).astype(BF16)
    step2u = [stage2a(1, step1u[0]), stage2b(1, step1u[1])]
    step3u = stage3(1, step2u)
    finish(0, step3c, gw_o)
    finish(1, step3u, gu_o)


def deliver(*refs):
    n = (len(refs) - 1) // 2
    copies = [pltpu.make_async_copy(refs[i], refs[n + i], refs[-1].at[i]) for i in range(n)]
    for c in copies:
        c.start()
    for c in copies:
        c.wait()


def local(dims, coarse, skip, up_weight, conv_weight, cotangent):
    XH, Y, Z, XL = dims
    NX, HL = XH * XL, CH // XL
    FB, CB = 9 * CH // (XH * Y * 2), CH // (Z * XL)
    RA = FB // 16 * 5 // 9 * 16
    RB = FB - RA
    FP = -(-FB // 128) * 128
    hbm, vmem = pl.BlockSpec(memory_space=pltpu.HBM), pl.BlockSpec(memory_space=pltpu.VMEM)
    V, dma = pltpu.VMEM, pltpu.SemaphoreType.DMA
    wide = V((9 * CH, CH), BF16)
    scratch = [
        V((RI, CJ, CH), BF16), V((2 * RI, 2 * CJ, CH), BF16), V((2 * RI, 2 * CJ, CH), BF16),
        wide, wide, wide, wide,
        V((2, 9 * AREA, 128), F32), V((2, 4 * CJ, 128), F32), V((2, 4 * CJ, 128), F32),
        V((2, 4 * AREA, 128), F32), V((2, 4 * AREA, 128), F32), V((4, 192, CH), F32), V((4, 64, CH), F32),
        V((4, 192, CH), BF16), V((4, 64, CH), BF16),
        V((8, 224, CH), BF16), V((8, 224, CH), BF16), V((8, 224, CH), BF16),
        V((192, 9 * CH), BF16), V((CH, 768), BF16), V((2, 4 * RI * CJ, 128), F32),
        V((4, 3, 16, CH), BF16), V((4, 5, 16, CH), BF16), V((4, 8, CH), F32),
        V((4, 3, 16, CH), BF16), V((4, 5, 16, CH), BF16), V((4, 8, CH), F32),
        V((2, XH, Y, 2, FB, CH), BF16), V((2, XH, Y, FB, CH), BF16), V((2, XH, Y, FB, CH), BF16),
        V((2, Y - 1, XH, RA, CH), BF16), V((2, NX - 1, Y, RB, HL), BF16),
        V((2, XH, RA, CH), F32), V((2, Y, RB, HL), F32), V((2, XH, RA, CH), BF16), V((2, Y, RB, HL), BF16),
        V((2, NX - 1, RA, HL), BF16), V((2, Y - 1, RB, HL), BF16),
        V((2, FP, HL), F32), V((2, Z, CB, FP), F32), V((2, Z, CB, FP), BF16), V((2, Z - 1, CB, FP), BF16),
        dma((5,)), dma((12,)), dma((12,)), dma((2,)), dma((2,)),
        dma((2, 2, 3)), dma((2, 2, 3)), dma((2, 2, 3)), dma((2, 2, 3)), dma((2, Z - 1)), dma((2, Z - 1)),
    ]
    shapes = (
        jax.ShapeDtypeStruct((2 * RI, 2 * CJ, CH), BF16),
        jax.ShapeDtypeStruct((RI * CJ, CH), BF16),
        jax.ShapeDtypeStruct((CB, FB), F32),
        jax.ShapeDtypeStruct((CB, FB), F32),
    )
    inputs = (coarse, skip, up_weight.reshape(9 * CH, CH), conv_weight.reshape(9 * CH, CH), cotangent)
    inputs = [pltpu.with_memory_space_constraint(x, pltpu.HBM) for x in inputs]
    results = pl.pallas_call(
        functools.partial(kernel, dims),
        out_shape=shapes,
        in_specs=[hbm] * 5,
        out_specs=(vmem,) * 4,
        scratch_shapes=scratch,
        compiler_params=pltpu.CompilerParams(
            collective_id=0, has_side_effects=True, vmem_limit_bytes=36 * 2**20
        ),
    )(*inputs)
    decoded, grad_coarse, grad_up, grad_conv = pl.pallas_call(
        deliver,
        out_shape=shapes,
        in_specs=[vmem] * 4,
        out_specs=(hbm,) * 4,
        scratch_shapes=[dma((4,))],
        compiler_params=pltpu.CompilerParams(vmem_limit_bytes=4 * 2**20),
    )(*results)
    return decoded, grad_coarse.reshape(RI, CJ, CH), grad_up.T, grad_conv.T


def build(mesh, dims):
    cells = P("band", "face", None)
    return jax.shard_map(
        functools.partial(local, dims),
        mesh=mesh,
        in_specs=(cells, cells, P(), P(), cells),
        out_specs=(cells, cells, P("face", "band"), P("face", "band")),
        check_vma=False,
    )


def solution(mesh):
    return build(mesh, (2, 4, 8, 2))
```

time: 47.2 us -> 41.6 us (0.88)
  local copies, waits for them, and re-layouts: 4.65 us -> 0 us
  Pallas kernels: 41.6 us -> 40.9 us
    unnamed x2 -> x0, local copies, waits for them, and re-layouts: 3.3 us -> none
    transpose x1 -> x0, local copies, waits for them, and re-layouts: 1.35 us -> none  [local(): grad_conv[:, :FB]]
    pallas_call x1 -> x2, Pallas kernels: 41.6 us -> 40.9 us  [the longest x1 40.1 us: local(): pl.pallas_call(functools.partial(kernel, dims), out_shape=shapes, in_spec...]
where the time goes in v2:
time: 41.6 us; the launch traced here: 41.5 us
  Pallas kernels  40.9 us (98%)
  between operations  0.64 us (2%)
    pallas_call x1, Pallas kernels, local(): pl.pallas_call(functools.partial(kernel, dims), out_shape=shapes, in_spec...  40.1 us

profile of v2, /device:TPU:1, one launch (start us, length us, event | category | flops | bytes accessed | tf_op | source)
XLA Modules:
  0.0 41.5 jit_solution(4347596235160745039)
XLA Ops:
  0.6 40.1 %shard_map.84 = (bf16[24,32,256]{2,1,0:T(8,128)(2,1)S(1)}, bf16[192,256]{1,0:T(8,128)(2,1)S(1)}, f32[16,144]{1,0:T(8,128)S(1)}, f32[16,144]{1,0:T(8,128)S(1)}) custom-call(bf16[12,16,256]{2,1,0:T(8,128)(2,1)} %coarse_h.1, bf16[24,32,256]{2,1,0:T(8,128)(2,1)} %skip_h.1, bf16[2304,256]{1,0:T(8,128)(2,1)} %bitcast.5, bf16[2304,256]{1,0:T(8,128)(2,1)} %bitcast.6, ...), custom_call_target="tpu_custom_call" | custom-call | tf_op jit(solution)/shard_map/pallas_call | solution.py:533
  40.7 0.8 %shard_map.85 = (bf16[24,32,256]{2,1,0:T(8,128)(2,1)}, bf16[192,256]{1,0:T(8,128)(2,1)}, f32[16,144]{1,0:T(8,128)}, f32[16,144]{1,0:T(8,128)}) custom-call(bf16[24,32,256]{2,1,0:T(8,128)(2,1)S(1)} %get-tuple-element.12.refs_0_, bf16[192,256]{1,0:T(8,128)(2,1)S(1)} %get-tuple-element.13.refs_1_, f32[16,144]{1,0:T(8,128)S(1)} %get-tuple-element.14.refs_2_, ...), custom_call_target="tpu_custom_call" | custom-call | tf_op jit(solution)/shard_map/pallas_call | solution.py:543

commit v3 on v2

--- a/solution.py
+++ b/solution.py
@@ -48,6 +48,10 @@
             ref[h, pl.ds(at, n), :] = part
         else:
             ref[h, pl.ds(at, n, stride=stride), :] = part
+
+
+def far(n):
+    return sorted(range(1, n), key=lambda d: (-min(d, n - d), d))
 
 
 def kernel(
@@ -77,38 +81,40 @@
     CB = CH // (Z * XL)
     nface, nband = XH * Y * 2, Z * XL
     face, band = lax.axis_index("face"), lax.axis_index("band")
-    core = face % 2
-    yy = (face // 2) % Y
-    xh = face // (2 * Y)
-    xl = band % XL
-    zz = band // XL
+    rem, div = lax.rem, lax.div
+    core = rem(face, 2)
+    yy = rem(div(face, 2), Y)
+    xh = div(face, 2 * Y)
+    xl = rem(band, XL)
+    zz = div(band, XL)
     xx = xh * XL + xl
 
     def dev(xx_, yy_, core_, zz_):
         return {
-            "face": (xx_ // XL) * (2 * Y) + yy_ * 2 + core_,
-            "band": zz_ * XL + xx_ % XL,
+            "face": div(xx_, XL) * (2 * Y) + yy_ * 2 + core_,
+            "band": zz_ * XL + rem(xx_, XL),
         }
 
     def near(di, dj):
-        return {"face": (face + dj + nface) % nface, "band": (band + di + nband) % nband}
+        return {"face": rem(face + dj + nface, nface), "band": rem(band + di + nband, nband)}
 
     def at_core():
         return dev(xx, yy, 1 - core, zz)
 
     def at_y(d):
-        return dev(xx, (yy + d) % Y, core, zz)
+        return dev(xx, rem(yy + d, Y), core, zz)
 
     def at_x(d):
-        return dev((xx + d) % NX, yy, core, zz)
+        return dev(rem(xx + d, NX), yy, core, zz)
 
     def at_z(d):
-        return dev(xx, yy, core, (zz + d) % Z)
+        return dev(xx, yy, core, rem(zz + d, Z))
 
     ways = [(-1, 0), (1, 0), (0, -1), (0, 1), (-1, -1), (-1, 1), (1, -1), (1, 1)]
-    partners = [near(*w) for w in ways] + [at_core()]
-    partners += [at_y(d) for d in range(1, Y)] + [at_x(d) for d in range(1, NX)]
-    partners += [at_z(d) for d in range(1, Z)]
+    far_z, far_y, far_x = far(Z), far(Y), far(NX)
+    partners = [near(*w) for w in ways[4:]] + [at_z(d) for d in far_z]
+    partners += [at_x(d) for d in far_x] + [at_y(d) for d in far_y]
+    partners += [near(*w) for w in ways[:4]] + [at_core()]
     barrier = pltpu.get_barrier_semaphore()
     for p in partners:
         pl.semaphore_signal(barrier, inc=1, device_id=p, device_id_type=MESH)
@@ -260,28 +266,20 @@
             ]
             start = stop
 
+    def first(arr, a):
+        c = remote(gsum.at[arr, a, :, 1 - core], r0.at[arr, a], s0s.at[arr, a], s0r.at[arr, a], at_core())
+        c.start()
+        return c
+
+    step0c = []
     for t, (k, l) in enumerate(TAPS):
         right = jnp.concatenate(
             [view(tvp, r - k + 1, s - l + 1, 0, RI) for r in range(2) for s in range(2)], axis=0
         )
         put(0, t, dot(actt[...], right).astype(BF16))
-
-    def first(arr):
-        return remote(
-            gsum.at[arr, :, :, 1 - core], r0.at[arr], s0s.at[arr], s0r.at[arr], at_core()
-        )
-
-    def second(arr):
-        def add(n, carry):
-            a, b = n // Y, n % Y
-            total = gsum[arr, a, b, core].astype(F32) + r0[arr, a, b].astype(F32)
-            s1[arr, a, b] = total.astype(BF16)
-            return carry
-
-        lax.fori_loop(0, XH * Y, add, 0)
-
-    step0c = first(0)
-    step0c.start()
+        if XH == 2 and t == 4:
+            step0c.append(first(0, 0))
+    step0c.append(first(0, XH - 1))
 
     for c in halo2:
         c.wait()
@@ -340,38 +338,44 @@
                 st(gf, ph * AREA + XC + 7, 16, side, XC)
 
     coarse_t = window(xf, 0, 0, 0, RI).T.astype(BF16)
+    step0u = []
     for t, (k, l) in enumerate(TAPS):
         (r, di), (s, dj) = split(k - 1), split(l - 1)
         part = window(gf, 2 * r + s, di, dj, RI).astype(BF16)
         gv[:, t * CH : (t + 1) * CH] = part
         put(1, t, dot(coarse_t, dot(part, perm).astype(BF16)).astype(BF16))
-    step0u = first(1)
-    step0u.start()
+        if XH == 2 and t == 4:
+            step0u.append(first(1, 0))
+    step0u.append(first(1, XH - 1))
 
     def half(x2):
-        return pl.ds(pl.multiple_of((x2 % XL) * HL, HL), HL)
-
-    def stage1(arr):
+        return pl.ds(pl.multiple_of(rem(x2, XL) * HL, HL), HL)
+
+    def stage1(arr, arrived):
         steps = [[], []]
-        for d in range(1, max(Y, NX)):
-            if d < Y:
+        for a in range(XH):
+            arrived[a].wait()
+            for b in range(Y):
+                total = gsum[arr, a, b, core].astype(F32) + r0[arr, a, b].astype(F32)
+                s1[arr, a, b] = total.astype(BF16)
+            for d in far_y:
                 q = Y - d - 1
                 steps[0].append(
                     remote(
-                        s1.at[arr, :, (yy + d) % Y, :RA], r1a.at[arr, q],
-                        s1s.at[arr, 0, d - 1], s1r.at[arr, 0, q], at_y(d),
+                        s1.at[arr, a, rem(yy + d, Y), :RA], r1a.at[arr, q, a],
+                        s1s.at[arr, a, d - 1], s1r.at[arr, a, q], at_y(d),
                     )
                 )
                 steps[0][-1].start()
-            if d < NX:
-                q, x2 = NX - d - 1, (xx + d) % NX
-                steps[1].append(
-                    remote(
-                        s1.at[arr, x2 // XL, :, RA:, half(x2)], r1b.at[arr, q],
-                        s1s.at[arr, 1, d - 1], s1r.at[arr, 1, q], at_x(d),
-                    )
+        for d in far_x:
+            q, x2 = NX - d - 1, rem(xx + d, NX)
+            steps[1].append(
+                remote(
+                    s1.at[arr, div(x2, XL), :, RA:, half(x2)], r1b.at[arr, q],
+                    s1s.at[arr, 2, d - 1], s1r.at[arr, 2, q], at_x(d),
                 )
-                steps[1][-1].start()
+            )
+            steps[1][-1].start()
         return steps
 
     def stage2a(arr, steps):
@@ -384,11 +388,11 @@
             a1a[arr, a] = total
             s2a[arr, a] = total.astype(BF16)
         out = []
-        for d in range(1, NX):
-            q, x2 = NX - d - 1, (xx + d) % NX
+        for d in far_x:
+            q, x2 = NX - d - 1, rem(xx + d, NX)
             out.append(
                 remote(
-                    s2a.at[arr, x2 // XL, :, half(x2)], r2a.at[arr, q],
+                    s2a.at[arr, div(x2, XL), :, half(x2)], r2a.at[arr, q],
                     s2s.at[arr, 0, d - 1], s2r.at[arr, 0, q], at_x(d),
                 )
             )
@@ -406,11 +410,11 @@
             a1b[arr, b] = total
             s2b[arr, b] = total.astype(BF16)
         out = []
-        for d in range(1, Y):
+        for d in far_y:
             q = Y - d - 1
             out.append(
                 remote(
-                    s2b.at[arr, (yy + d) % Y], r2b.at[arr, q],
+                    s2b.at[arr, rem(yy + d, Y)], r2b.at[arr, q],
                     s2s.at[arr, 1, d - 1], s2r.at[arr, 1, q], at_y(d),
                 )
             )
@@ -435,10 +439,10 @@
             a3[arr, z] = turned[z * CB : (z + 1) * CB]
             s3[arr, z] = turned[z * CB : (z + 1) * CB].astype(BF16)
         out = []
-        for d in range(1, Z):
+        for d in far_z:
             q = Z - d - 1
             out.append(
-                remote(s3.at[arr, (zz + d) % Z], r3.at[arr, q], s3s.at[arr, d - 1], s3r.at[arr, q], at_z(d))
+                remote(s3.at[arr, rem(zz + d, Z)], r3.at[arr, q], s3s.at[arr, d - 1], s3r.at[arr, q], at_z(d))
             )
             out[-1].start()
         return out
@@ -457,29 +461,26 @@
         for i in range(RI):
             st(dec_v, (2 * i + r) * 2 * CJ + s, CJ, out[16 * i : 16 * i + 16], 2)
 
-    step0c.wait()
-    second(0)
-    step1c = stage1(0)
+    step1c = stage1(0, step0c)
 
     for r in range(2):
         for s in range(2):
             for v, dj in enumerate((0, 1 if s == 0 else -1)):
                 av[(2 * r + s) * 2 + v] = window(af, 2 * r + s, -1, dj, 14).astype(BF16)
 
-    step0u.wait()
-    second(1)
-    step1u = stage1(1)
+    step1u = stage1(1, step0u)
 
     decode(0, 0)
     decode(0, 1)
-    step2c = [stage2a(0, step1c[0]), stage2b(0, step1c[1])]
     decode(1, 0)
     decode(1, 1)
-    step3c = stage3(0, step2c)
     gc_o[...] = dot(gv[...], upwt[...]).astype(BF16)
     for p in range(2 * RI):
         dec_o[p] = ld(dec_v, p * 2 * CJ, 2 * CJ).astype(BF16)
+
+    step2c = [stage2a(0, step1c[0]), stage2b(0, step1c[1])]
     step2u = [stage2a(1, step1u[0]), stage2b(1, step1u[1])]
+    step3c = stage3(0, step2c)
     step3u = stage3(1, step2u)
     finish(0, step3c, gw_o)
     finish(1, step3u, gu_o)
@@ -519,8 +520,8 @@
         V((2, XH, RA, CH), F32), V((2, Y, RB, HL), F32), V((2, XH, RA, CH), BF16), V((2, Y, RB, HL), BF16),
         V((2, NX - 1, RA, HL), BF16), V((2, Y - 1, RB, HL), BF16),
         V((2, FP, HL), F32), V((2, Z, CB, FP), F32), V((2, Z, CB, FP), BF16), V((2, Z - 1, CB, FP), BF16),
-        dma((5,)), dma((12,)), dma((12,)), dma((2,)), dma((2,)),
-        dma((2, 2, 3)), dma((2, 2, 3)), dma((2, 2, 3)), dma((2, 2, 3)), dma((2, Z - 1)), dma((2, Z - 1)),
+        dma((5,)), dma((12,)), dma((12,)), dma((2, 2)), dma((2, 2)),
+        dma((2, 3, 3)), dma((2, 3, 3)), dma((2, 2, 3)), dma((2, 2, 3)), dma((2, Z - 1)), dma((2, Z - 1)),
     ]
     shapes = (
         jax.ShapeDtypeStruct((2 * RI, 2 * CJ, CH), BF16),

time: 41.6 us -> 39.3 us (0.945)
  Pallas kernels: 40.9 us -> 38.5 us
    pallas_call x1, Pallas kernels: 40.1 us -> 37.7 us  [local(): pl.pallas_call(functools.partial(kernel, dims), out_shape=shapes, in_spec...]
where the time goes in v3:
time: 39.3 us; the launch traced here: 39.2 us
  Pallas kernels  38.5 us (98%)
  between operations  0.64 us (2%)
    pallas_call x1, Pallas kernels, local(): pl.pallas_call(functools.partial(kernel, dims), out_shape=shapes, in_spec...  37.7 us
    pallas_call x1, Pallas kernels, local(): pl.pallas_call(deliver, out_shape=shapes, in_specs=[vmem] * 4, out_specs=...  0.81 us

profile of v3, /device:TPU:1, one launch (start us, length us, event | category | flops | bytes accessed | tf_op | source)
XLA Modules:
  0.0 39.2 jit_solution(14965272414449138794)
XLA Ops:
  0.6 37.7 %shard_map.84 = (bf16[24,32,256]{2,1,0:T(8,128)(2,1)S(1)}, bf16[192,256]{1,0:T(8,128)(2,1)S(1)}, f32[16,144]{1,0:T(8,128)S(1)}, f32[16,144]{1,0:T(8,128)S(1)}) custom-call(bf16[12,16,256]{2,1,0:T(8,128)(2,1)} %coarse_h.1, bf16[24,32,256]{2,1,0:T(8,128)(2,1)} %skip_h.1, bf16[2304,256]{1,0:T(8,128)(2,1)} %bitcast.5, bf16[2304,256]{1,0:T(8,128)(2,1)} %bitcast.6, ...), custom_call_target="tpu_custom_call" | custom-call | tf_op jit(solution)/shard_map/pallas_call | solution.py:534
  38.4 0.8 %shard_map.85 = (bf16[24,32,256]{2,1,0:T(8,128)(2,1)}, bf16[192,256]{1,0:T(8,128)(2,1)}, f32[16,144]{1,0:T(8,128)}, f32[16,144]{1,0:T(8,128)}) custom-call(bf16[24,32,256]{2,1,0:T(8,128)(2,1)S(1)} %get-tuple-element.12.refs_0_, bf16[192,256]{1,0:T(8,128)(2,1)S(1)} %get-tuple-element.13.refs_1_, f32[16,144]{1,0:T(8,128)S(1)} %get-tuple-element.14.refs_2_, ...), custom_call_target="tpu_custom_call" | custom-call | tf_op jit(solution)/shard_map/pallas_call | solution.py:544

commit v4 on v3

--- a/solution.py
+++ b/solution.py
@@ -59,7 +59,7 @@
     coarse_h, skip_h, upw_h, convw_h, cot_h,
     dec_o, gc_o, gu_o, gw_o,
     coarse_v, skip_v, cot_v, upw, convw, upwt, convwt,
-    xf, fs, ft, af, gf, dfac, dghost, ce, cg, tv, tvp, av, gv, actt, dec_v,
+    xf, fs, ft, af, gf, dfac, dghost, ce, cg, cet, gpp, gb, tv, tvp, av, gv, actt, dec_v,
     m_1, m_2, m_co, r_1, r_2, r_co,
     gsum, r0, s1, r1a, r1b, a1a, a1b, s2a, s2b, r2a, r2b, pad, a3, s3, r3,
     in_sem, hs, hr, s0s, s0r, s1s, s1r, s2s, s2r, s3s, s3r,
@@ -170,15 +170,6 @@
         )
     for c in halo1:
         c.start()
-    for way, fields in enumerate((UP2, DOWN2, LEFT2, RIGHT2)):
-        message(m_2, fields, way)
-        n = len(fields)
-        halo2.append(
-            remote(m_2.at[way, :n], r_2.at[way, :n], hs.at[8 + way], hr.at[8 + way], near(*ways[way]))
-        )
-    for c in halo2:
-        c.start()
-
     for c in loads[3:]:
         c.wait()
 
@@ -207,8 +198,16 @@
             else:
                 st(xf, a * AREA + 2 * XC + (8 + CJ if way == 2 else 7), RI, value[:RI], XC)
 
+    for way, fields in enumerate((UP2, DOWN2, LEFT2, RIGHT2)):
+        message(m_2, fields, way)
+        n = len(fields)
+        halo2.append(
+            remote(m_2.at[way, :n], r_2.at[way, :n], hs.at[8 + way], hr.at[8 + way], near(*ways[way]))
+        )
     for c in halo1:
         c.wait()
+    for c in halo2:
+        c.start()
     for way, fields in enumerate((UP1, DOWN1, LEFT1, RIGHT1)):
         receive(r_1, fields, way)
     for m, (di, dj, fields) in enumerate(CORNERS):
@@ -280,73 +279,6 @@
         if XH == 2 and t == 4:
             step0c.append(first(0, 0))
     step0c.append(first(0, XH - 1))
-
-    for c in halo2:
-        c.wait()
-    for way, fields in enumerate((UP2, DOWN2, LEFT2, RIGHT2)):
-        receive(r_2, fields, way)
-
-    def border(a, di, dj):
-        return jnp.concatenate(
-            [window(xf, a, di - 1, dj, 1), window(xf, a, di + RI, dj, 1)]
-            + [rows(a, di - 1, dj - 1, 16), rows(a, di - 1, dj + CJ, 16)],
-            axis=0,
-        )
-
-    for di in range(2):
-        for dj in range(2):
-            cg[2 * di + dj] = border(0, di, dj).astype(BF16)
-    line = lax.broadcasted_iota(jnp.int32, (64, CH), 0)
-    first_row = (line < 16) | ((line >= 32) & (line % 16 == 0))
-    last_row = ((line >= 16) & (line < 32)) | ((line >= 32) & (line % 16 == RI + 1))
-    ghost = ((band == 0) & first_row) | ((band == nband - 1) & last_row)
-    for r in range(2):
-        for s in range(2):
-            ph = 2 * r + s
-            pre = up(cg, r, s) + border(1 + ph, 0, 0)
-            sig = jax.nn.sigmoid(pre)
-            act = jnp.where(ghost, 0.0, pre * sig).astype(BF16).astype(F32)
-            dghost[ph] = jnp.where(ghost, 0.0, sig * (1.0 + pre * (1.0 - sig)))
-            st(af, ph * AREA + XC + 8, CJ, act[:16])
-            st(af, ph * AREA + (RI + 2) * XC + 8, CJ, act[16:32])
-            st(af, ph * AREA + XC + 7, 16, act[32:48], XC)
-            st(af, ph * AREA + XC + 8 + CJ, 16, act[48:], XC)
-
-    for s in range(2):
-        for v, dj in enumerate((0, 1 if s == 0 else -1)):
-            tv[2 * s + v, :16] = window(xf, 5 + s, -1, dj, 1).astype(BF16)
-
-    for r in range(2):
-        for s in range(2):
-            ph = 2 * r + s
-            i0 = -1 if r else 0
-            n = RI - i0
-            left = jnp.concatenate([view(tv, r - k + 1, s - l + 1, i0, n) for k, l in TAPS], axis=1)
-            if s:
-                column = []
-                for k, l in TAPS:
-                    (r2, di), (s2, dj) = split(r - k + 1), split(s - l + 1)
-                    column.append(rows(5 + 2 * r2 + s2, -1 + di, -1 + dj, 16).astype(BF16))
-                left = jnp.concatenate([left, jnp.concatenate(column, axis=1)], axis=0)
-            grad = dot(left, convwt[...])
-            slope = jnp.concatenate([dghost[ph, :16], dfac[ph]], axis=0) if r else dfac[ph]
-            main = (grad[: 16 * n] * slope).astype(BF16).astype(F32)
-            for q in range(n):
-                st(gf, ph * AREA + (i0 + q + 2) * XC + 8, CJ, main[16 * q : 16 * q + 16])
-            if s:
-                side = (grad[16 * n :] * dghost[ph, 32:48]).astype(BF16).astype(F32)
-                st(gf, ph * AREA + XC + 7, 16, side, XC)
-
-    coarse_t = window(xf, 0, 0, 0, RI).T.astype(BF16)
-    step0u = []
-    for t, (k, l) in enumerate(TAPS):
-        (r, di), (s, dj) = split(k - 1), split(l - 1)
-        part = window(gf, 2 * r + s, di, dj, RI).astype(BF16)
-        gv[:, t * CH : (t + 1) * CH] = part
-        put(1, t, dot(coarse_t, dot(part, perm).astype(BF16)).astype(BF16))
-        if XH == 2 and t == 4:
-            step0u.append(first(1, 0))
-    step0u.append(first(1, XH - 1))
 
     def half(x2):
         return pl.ds(pl.multiple_of(rem(x2, XL) * HL, HL), HL)
@@ -378,6 +310,38 @@
             steps[1][-1].start()
         return steps
 
+    phases = [(r, s) for r in range(2) for s in range(2)]
+
+    def stacked(ref, step, group):
+        return jnp.concatenate(
+            [
+                jnp.concatenate([view(ref, *step(r, s, k, l), 0, RI) for r, s in group], axis=0)
+                for k, l in TAPS
+            ],
+            axis=1,
+        )
+
+    for g in range(0, 4, 4):
+        group = phases[g : g + 4]
+        left = stacked(tv, lambda r, s, k, l: (r - k + 1, s - l + 1), group)
+        grads = dot(left, convwt[...])
+        for n, (r, s) in enumerate(group):
+            ph = 2 * r + s
+            grad = (grads[192 * n : 192 * n + 192] * dfac[ph]).astype(BF16)
+            gpp[ph] = dot(grad, perm).astype(BF16)
+            gb[ph] = grad
+
+    for n in range(4):
+        cet[n] = window(xf, 0, n // 2, n % 2, RI).T.astype(BF16)
+    step1c = stage1(0, step0c)
+    step0u = []
+    for t, (k, l) in enumerate(TAPS):
+        (r, di), (s, dj) = (((1, 1), (0, 0), (1, 0))[m] for m in (k, l))
+        put(1, t, dot(cet[2 * di + dj], gpp[2 * r + s]).astype(BF16))
+        if XH == 2 and t == 4:
+            step0u.append(first(1, 0))
+    step0u.append(first(1, XH - 1))
+
     def stage2a(arr, steps):
         for c in steps:
             c.wait()
@@ -455,25 +419,81 @@
             total = total + r3[arr, d].astype(F32)
         out[...] = total[:, :FB]
 
-    def decode(r, s):
-        left = jnp.concatenate([view(av, r + k - 1, s + l - 1, 0, RI) for k, l in TAPS], axis=1)
-        out = dot(left, convw[...])
-        for i in range(RI):
-            st(dec_v, (2 * i + r) * 2 * CJ + s, CJ, out[16 * i : 16 * i + 16], 2)
-
-    step1c = stage1(0, step0c)
+    def decode(group):
+        outs = dot(stacked(av, lambda r, s, k, l: (r + k - 1, s + l - 1), group), convw[...])
+        for n, (r, s) in enumerate(group):
+            out = outs[192 * n : 192 * n + 192]
+            for i in range(RI):
+                st(dec_v, (2 * i + r) * 2 * CJ + s, CJ, out[16 * i : 16 * i + 16], 2)
+
+    step1u = stage1(1, step0u)
+
+    for c in halo2:
+        c.wait()
+    for way, fields in enumerate((UP2, DOWN2, LEFT2, RIGHT2)):
+        receive(r_2, fields, way)
+
+    def border(a, di, dj):
+        return jnp.concatenate(
+            [window(xf, a, di - 1, dj, 1), window(xf, a, di + RI, dj, 1)]
+            + [rows(a, di - 1, dj - 1, 16), rows(a, di - 1, dj + CJ, 16)],
+            axis=0,
+        )
+
+    for di in range(2):
+        for dj in range(2):
+            cg[2 * di + dj] = border(0, di, dj).astype(BF16)
+    line = lax.broadcasted_iota(jnp.int32, (64, CH), 0)
+    first_row = (line < 16) | ((line >= 32) & (line % 16 == 0))
+    last_row = ((line >= 16) & (line < 32)) | ((line >= 32) & (line % 16 == RI + 1))
+    ghost = ((band == 0) & first_row) | ((band == nband - 1) & last_row)
+    for r in range(2):
+        for s in range(2):
+            ph = 2 * r + s
+            pre = up(cg, r, s) + border(1 + ph, 0, 0)
+            sig = jax.nn.sigmoid(pre)
+            act = jnp.where(ghost, 0.0, pre * sig).astype(BF16).astype(F32)
+            dghost[ph] = jnp.where(ghost, 0.0, sig * (1.0 + pre * (1.0 - sig)))
+            st(af, ph * AREA + XC + 8, CJ, act[:16])
+            st(af, ph * AREA + (RI + 2) * XC + 8, CJ, act[16:32])
+            st(af, ph * AREA + XC + 7, 16, act[32:48], XC)
+            st(af, ph * AREA + XC + 8 + CJ, 16, act[48:], XC)
+
+    for s in range(2):
+        for v, dj in enumerate((0, 1 if s == 0 else -1)):
+            tv[2 * s + v, :16] = window(xf, 5 + s, -1, dj, 1).astype(BF16)
 
     for r in range(2):
         for s in range(2):
             for v, dj in enumerate((0, 1 if s == 0 else -1)):
                 av[(2 * r + s) * 2 + v] = window(af, 2 * r + s, -1, dj, 14).astype(BF16)
 
-    step1u = stage1(1, step0u)
-
-    decode(0, 0)
-    decode(0, 1)
-    decode(1, 0)
-    decode(1, 1)
+    for ph in range(4):
+        grad = gb[ph].astype(F32)
+        for q in range(RI):
+            st(gf, ph * AREA + (q + 2) * XC + 8, CJ, grad[16 * q : 16 * q + 16])
+    lines, slopes = [], []
+    for s in range(2):
+        lines.append(jnp.concatenate([view(tv, 2 - k, s - l + 1, -1, 1) for k, l in TAPS], axis=1))
+        slopes.append(dghost[2 + s, :16])
+    for r in range(2):
+        column = []
+        for k, l in TAPS:
+            (r2, di), (s2, dj) = split(r - k + 1), split(2 - l)
+            column.append(rows(5 + 2 * r2 + s2, -1 + di, -1 + dj, 16).astype(BF16))
+        lines.append(jnp.concatenate(column, axis=1))
+        slopes.append(dghost[2 * r + 1, 32:48])
+    grad = dot(jnp.concatenate(lines, axis=0), convwt[...]) * jnp.concatenate(slopes, axis=0)
+    grad = grad.astype(BF16).astype(F32)
+    st(gf, 2 * AREA + XC + 8, CJ, grad[:16])
+    st(gf, 3 * AREA + XC + 8, CJ, grad[16:32])
+    st(gf, AREA + XC + 7, 16, grad[32:48], XC)
+    st(gf, 3 * AREA + XC + 7, 16, grad[48:], XC)
+    for t, (k, l) in enumerate(TAPS):
+        (r, di), (s, dj) = split(k - 1), split(l - 1)
+        gv[:, t * CH : (t + 1) * CH] = window(gf, 2 * r + s, di, dj, RI).astype(BF16)
+
+    decode(phases[0:4])
     gc_o[...] = dot(gv[...], upwt[...]).astype(BF16)
     for p in range(2 * RI):
         dec_o[p] = ld(dec_v, p * 2 * CJ, 2 * CJ).astype(BF16)
@@ -510,7 +530,7 @@
         wide, wide, wide, wide,
         V((2, 9 * AREA, 128), F32), V((2, 4 * CJ, 128), F32), V((2, 4 * CJ, 128), F32),
         V((2, 4 * AREA, 128), F32), V((2, 4 * AREA, 128), F32), V((4, 192, CH), F32), V((4, 64, CH), F32),
-        V((4, 192, CH), BF16), V((4, 64, CH), BF16),
+        V((4, 192, CH), BF16), V((4, 64, CH), BF16), V((4, CH, 192), BF16), V((4, 192, CH), BF16), V((4, 192, CH), BF16),
         V((8, 224, CH), BF16), V((8, 224, CH), BF16), V((8, 224, CH), BF16),
         V((192, 9 * CH), BF16), V((CH, 768), BF16), V((2, 4 * RI * CJ, 128), F32),
         V((4, 3, 16, CH), BF16), V((4, 5, 16, CH), BF16), V((4, 8, CH), F32),

time: 39.3 us -> 38.4 us (0.977)
  Pallas kernels: 38.5 us -> 37.7 us
    pallas_call x1, Pallas kernels: 37.7 us -> 36.9 us  [local(): pl.pallas_call(functools.partial(kernel, dims), out_shape=shapes, in_spec...]
where the time goes in v4:
time: 38.4 us; the launch traced here: 38.3 us
  Pallas kernels  37.7 us (98%)
  between operations  0.64 us (2%)
    pallas_call x1, Pallas kernels, local(): pl.pallas_call(functools.partial(kernel, dims), out_shape=shapes, in_spec...  36.9 us
    pallas_call x1, Pallas kernels, local(): pl.pallas_call(deliver, out_shape=shapes, in_specs=[vmem] * 4, out_specs=...  0.81 us

profile of v4, /device:TPU:1, one launch (start us, length us, event | category | flops | bytes accessed | tf_op | source)
XLA Modules:
  0.0 38.3 jit_solution(10272990522704824773)
XLA Ops:
  0.6 36.9 %shard_map.84 = (bf16[24,32,256]{2,1,0:T(8,128)(2,1)S(1)}, bf16[192,256]{1,0:T(8,128)(2,1)S(1)}, f32[16,144]{1,0:T(8,128)S(1)}, f32[16,144]{1,0:T(8,128)S(1)}) custom-call(bf16[12,16,256]{2,1,0:T(8,128)(2,1)} %coarse_h.1, bf16[24,32,256]{2,1,0:T(8,128)(2,1)} %skip_h.1, bf16[2304,256]{1,0:T(8,128)(2,1)} %bitcast.5, bf16[2304,256]{1,0:T(8,128)(2,1)} %bitcast.6, ...), custom_call_target="tpu_custom_call" | custom-call | tf_op jit(solution)/shard_map/pallas_call | solution.py:554
  37.5 0.8 %shard_map.85 = (bf16[24,32,256]{2,1,0:T(8,128)(2,1)}, bf16[192,256]{1,0:T(8,128)(2,1)}, f32[16,144]{1,0:T(8,128)}, f32[16,144]{1,0:T(8,128)}) custom-call(bf16[24,32,256]{2,1,0:T(8,128)(2,1)S(1)} %get-tuple-element.12.refs_0_, bf16[192,256]{1,0:T(8,128)(2,1)S(1)} %get-tuple-element.13.refs_1_, f32[16,144]{1,0:T(8,128)S(1)} %get-tuple-element.14.refs_2_, ...), custom_call_target="tpu_custom_call" | custom-call | tf_op jit(solution)/shard_map/pallas_call | solution.py:564

commit v5 on v4

--- a/solution.py
+++ b/solution.py
@@ -204,6 +204,42 @@
         halo2.append(
             remote(m_2.at[way, :n], r_2.at[way, :n], hs.at[8 + way], hr.at[8 + way], near(*ways[way]))
         )
+    def window(ref, a, i, dj, n):
+        return jnp.concatenate(
+            [ld(ref, a * AREA + (i + q + 2) * XC + 8 + dj, CJ) for q in range(n)], axis=0
+        )
+
+    def up(left, r, s):
+        terms = []
+        for k, di in ((1, 0),) if r == 0 else ((2, 0), (0, 1)):
+            for l, dj in ((1, 0),) if s == 0 else ((2, 0), (0, 1)):
+                terms.append((2 * di + dj, (3 * k + l) * CH))
+        terms = [lambda n=n, at=at: dot(left[n], upw[at : at + CH, :]) for n, at in terms]
+        return terms[0], sum((term() for term in terms[1:]), 0.0)
+
+    def activate(r, s, pre):
+        ph = 2 * r + s
+        sig = jax.nn.sigmoid(pre)
+        act = (pre * sig).astype(BF16).astype(F32)
+        dfac[ph] = sig * (1.0 + pre * (1.0 - sig))
+        for q in range(RI):
+            st(af, ph * AREA + (q + 2) * XC + 8, CJ, act[16 * q : 16 * q + 16])
+        actt[:, ph * 192 : ph * 192 + 192] = act.T.astype(BF16)
+
+    ce[0] = window(xf, 0, 0, 0, RI).astype(BF16)
+    cet[0] = window(xf, 0, 0, 0, RI).T.astype(BF16)
+    for r in range(2):
+        for s in range(2):
+            ph = 2 * r + s
+            at = (3 * (1 + r) + 1 + s) * CH
+            own = dot(ce[0], upw[at : at + CH, :]) + window(xf, 1 + ph, 0, 0, RI)
+            if ph:
+                dfac[ph] = own
+            else:
+                activate(0, 0, own)
+            tv[2 * ph] = window(xf, 5 + ph, -1, 0, 14).astype(BF16)
+            tvp[2 * ph] = dot(tv[2 * ph], perm).astype(BF16)
+
     for c in halo1:
         c.wait()
     for c in halo2:
@@ -216,39 +252,22 @@
             at = a * AREA + (RI + 2 if di < 0 else 1) * XC + (8 + CJ if dj < 0 else 7)
             st(xf, at, 1, r_co[m, n : n + 1] * keep)
 
-    def window(ref, a, i, dj, n):
-        return jnp.concatenate(
-            [ld(ref, a * AREA + (i + q + 2) * XC + 8 + dj, CJ) for q in range(n)], axis=0
-        )
-
-    def up(left, r, s):
-        total = None
-        for k, di in ((1, 0),) if r == 0 else ((2, 0), (0, 1)):
-            for l, dj in ((1, 0),) if s == 0 else ((2, 0), (0, 1)):
-                term = dot(left[2 * di + dj], upw[(3 * k + l) * CH : (3 * k + l + 1) * CH, :])
-                total = term if total is None else total + term
-        return total
-
-    for di in range(2):
-        for dj in range(2):
-            ce[2 * di + dj] = window(xf, 0, di, dj, RI).astype(BF16)
-    for r in range(2):
-        for s in range(2):
-            ph = 2 * r + s
-            pre = up(ce, r, s) + window(xf, 1 + ph, 0, 0, RI)
-            sig = jax.nn.sigmoid(pre)
-            act = (pre * sig).astype(BF16).astype(F32)
-            dfac[ph] = sig * (1.0 + pre * (1.0 - sig))
-            for q in range(RI):
-                st(af, ph * AREA + (q + 2) * XC + 8, CJ, act[16 * q : 16 * q + 16])
-            actt[:, ph * 192 : ph * 192 + 192] = act.T.astype(BF16)
-
-    for r in range(2):
-        for s in range(2):
-            for v, dj in enumerate((0, 1 if s == 0 else -1)):
-                n = (2 * r + s) * 2 + v
-                tv[n] = window(xf, 5 + 2 * r + s, -1, dj, 14).astype(BF16)
-                tvp[n] = dot(tv[n], perm).astype(BF16)
+    for n in range(1, 4):
+        ce[n] = window(xf, 0, n // 2, n % 2, RI).astype(BF16)
+    for r, s in ((0, 1), (1, 0), (1, 1)):
+        activate(r, s, dfac[2 * r + s] + up(ce, r, s)[1])
+
+    ends = []
+    for ph in range(4):
+        for i in (-1, RI):
+            ends.append(window(xf, 5 + ph, i, 0, 1).astype(BF16))
+            tv[2 * ph, 16 * (i + 1) : 16 * (i + 2)] = ends[-1]
+    ends = dot(jnp.concatenate(ends, axis=0), perm).astype(BF16)
+    for ph in range(4):
+        for m, i in enumerate((-1, RI)):
+            tvp[2 * ph, 16 * (i + 1) : 16 * (i + 2)] = ends[16 * (2 * ph + m) : 16 * (2 * ph + m + 1)]
+        tv[2 * ph + 1] = window(xf, 5 + ph, -1, 1 if ph % 2 == 0 else -1, 14).astype(BF16)
+        tvp[2 * ph + 1] = dot(tv[2 * ph + 1], perm).astype(BF16)
 
     def view(ref, er, es, i0, n):
         (r, di), (s, dj) = split(er), split(es)
@@ -276,7 +295,7 @@
             [view(tvp, r - k + 1, s - l + 1, 0, RI) for r in range(2) for s in range(2)], axis=0
         )
         put(0, t, dot(actt[...], right).astype(BF16))
-        if XH == 2 and t == 4:
+        if XH == 2 and t == 6:
             step0c.append(first(0, 0))
     step0c.append(first(0, XH - 1))
 
@@ -288,8 +307,7 @@
         for a in range(XH):
             arrived[a].wait()
             for b in range(Y):
-                total = gsum[arr, a, b, core].astype(F32) + r0[arr, a, b].astype(F32)
-                s1[arr, a, b] = total.astype(BF16)
+                s1[arr, a, b] = gsum[arr, a, b, core] + r0[arr, a, b]
             for d in far_y:
                 q = Y - d - 1
                 steps[0].append(
@@ -331,14 +349,14 @@
             gpp[ph] = dot(grad, perm).astype(BF16)
             gb[ph] = grad
 
-    for n in range(4):
+    for n in range(1, 4):
         cet[n] = window(xf, 0, n // 2, n % 2, RI).T.astype(BF16)
     step1c = stage1(0, step0c)
     step0u = []
     for t, (k, l) in enumerate(TAPS):
         (r, di), (s, dj) = (((1, 1), (0, 0), (1, 0))[m] for m in (k, l))
         put(1, t, dot(cet[2 * di + dj], gpp[2 * r + s]).astype(BF16))
-        if XH == 2 and t == 4:
+        if XH == 2 and t == 6:
             step0u.append(first(1, 0))
     step0u.append(first(1, XH - 1))
 
@@ -450,7 +468,8 @@
     for r in range(2):
         for s in range(2):
             ph = 2 * r + s
-            pre = up(cg, r, s) + border(1 + ph, 0, 0)
+            own, others = up(cg, r, s)
+            pre = own() + others + border(1 + ph, 0, 0)
             sig = jax.nn.sigmoid(pre)
             act = jnp.where(ghost, 0.0, pre * sig).astype(BF16).astype(F32)
             dghost[ph] = jnp.where(ghost, 0.0, sig * (1.0 + pre * (1.0 - sig)))

time: 38.4 us -> 38.3 us (level)
  no operation moved by 1% of the time
where the time goes in v5:
time: 38.3 us; the launch traced here: 38.2 us
  Pallas kernels  37.6 us (98%)
  between operations  0.64 us (2%)
    pallas_call x1, Pallas kernels, local(): pl.pallas_call(functools.partial(kernel, dims), out_shape=shapes, in_spec...  36.8 us
    pallas_call x1, Pallas kernels, local(): pl.pallas_call(deliver, out_shape=shapes, in_specs=[vmem] * 4, out_specs=...  0.81 us

profile of v5, /device:TPU:1, one launch (start us, length us, event | category | flops | bytes accessed | tf_op | source)
XLA Modules:
  0.0 38.2 jit_solution(6023336111818176922)
XLA Ops:
  0.6 36.8 %shard_map.84 = (bf16[24,32,256]{2,1,0:T(8,128)(2,1)S(1)}, bf16[192,256]{1,0:T(8,128)(2,1)S(1)}, f32[16,144]{1,0:T(8,128)S(1)}, f32[16,144]{1,0:T(8,128)S(1)}) custom-call(bf16[12,16,256]{2,1,0:T(8,128)(2,1)} %coarse_h.1, bf16[24,32,256]{2,1,0:T(8,128)(2,1)} %skip_h.1, bf16[2304,256]{1,0:T(8,128)(2,1)} %bitcast.5, bf16[2304,256]{1,0:T(8,128)(2,1)} %bitcast.6, ...), custom_call_target="tpu_custom_call" | custom-call | tf_op jit(solution)/shard_map/pallas_call | solution.py:573
  37.4 0.8 %shard_map.85 = (bf16[24,32,256]{2,1,0:T(8,128)(2,1)}, bf16[192,256]{1,0:T(8,128)(2,1)}, f32[16,144]{1,0:T(8,128)}, f32[16,144]{1,0:T(8,128)}) custom-call(bf16[24,32,256]{2,1,0:T(8,128)(2,1)S(1)} %get-tuple-element.12.refs_0_, bf16[192,256]{1,0:T(8,128)(2,1)S(1)} %get-tuple-element.13.refs_1_, f32[16,144]{1,0:T(8,128)S(1)} %get-tuple-element.14.refs_2_, ...), custom_call_target="tpu_custom_call" | custom-call | tf_op jit(solution)/shard_map/pallas_call | solution.py:583

commit v6 on v5

--- a/solution.py
+++ b/solution.py
@@ -77,7 +77,7 @@
     NX = XH * XL
     HL = CH // XL
     FB = 9 * CH // (XH * Y * 2)
-    RA = FB // 16 * 5 // 9 * 16
+    RA = FB // 16 * 6 // 9 * 16
     CB = CH // (Z * XL)
     nface, nband = XH * Y * 2, Z * XL
     face, band = lax.axis_index("face"), lax.axis_index("band")
@@ -538,7 +538,7 @@
     XH, Y, Z, XL = dims
     NX, HL = XH * XL, CH // XL
     FB, CB = 9 * CH // (XH * Y * 2), CH // (Z * XL)
-    RA = FB // 16 * 5 // 9 * 16
+    RA = FB // 16 * 6 // 9 * 16
     RB = FB - RA
     FP = -(-FB // 128) * 128
     hbm, vmem = pl.BlockSpec(memory_space=pltpu.HBM), pl.BlockSpec(memory_space=pltpu.VMEM)

time: 38.3 us -> 39.6 us (1.034)
  Pallas kernels: 37.6 us -> 38.9 us
    pallas_call x1, Pallas kernels: 36.8 us -> 38.1 us  [local(): pl.pallas_call(functools.partial(kernel, dims), out_shape=shapes, in_spec...]
where the time goes in v6:
time: 39.6 us; the launch traced here: 39.5 us
  Pallas kernels  38.9 us (98%)
  between operations  0.64 us (2%)
    pallas_call x1, Pallas kernels, local(): pl.pallas_call(functools.partial(kernel, dims), out_shape=shapes, in_spec...  38.1 us
    pallas_call x1, Pallas kernels, local(): pl.pallas_call(deliver, out_shape=shapes, in_specs=[vmem] * 4, out_specs=...  0.81 us

profile of v6, /device:TPU:1, one launch (start us, length us, event | category | flops | bytes accessed | tf_op | source)
XLA Modules:
  0.0 39.5 jit_solution(6527954841928485576)
XLA Ops:
  0.6 38.1 %shard_map.84 = (bf16[24,32,256]{2,1,0:T(8,128)(2,1)S(1)}, bf16[192,256]{1,0:T(8,128)(2,1)S(1)}, f32[16,144]{1,0:T(8,128)S(1)}, f32[16,144]{1,0:T(8,128)S(1)}) custom-call(bf16[12,16,256]{2,1,0:T(8,128)(2,1)} %coarse_h.1, bf16[24,32,256]{2,1,0:T(8,128)(2,1)} %skip_h.1, bf16[2304,256]{1,0:T(8,128)(2,1)} %bitcast.5, bf16[2304,256]{1,0:T(8,128)(2,1)} %bitcast.6, ...), custom_call_target="tpu_custom_call" | custom-call | tf_op jit(solution)/shard_map/pallas_call | solution.py:573
  38.7 0.8 %shard_map.85 = (bf16[24,32,256]{2,1,0:T(8,128)(2,1)}, bf16[192,256]{1,0:T(8,128)(2,1)}, f32[16,144]{1,0:T(8,128)}, f32[16,144]{1,0:T(8,128)}) custom-call(bf16[24,32,256]{2,1,0:T(8,128)(2,1)S(1)} %get-tuple-element.12.refs_0_, bf16[192,256]{1,0:T(8,128)(2,1)S(1)} %get-tuple-element.13.refs_1_, f32[16,144]{1,0:T(8,128)S(1)} %get-tuple-element.14.refs_2_, ...), custom_call_target="tpu_custom_call" | custom-call | tf_op jit(solution)/shard_map/pallas_call | solution.py:583

commit v7 on v6

--- a/solution.py
+++ b/solution.py
@@ -77,7 +77,7 @@
     NX = XH * XL
     HL = CH // XL
     FB = 9 * CH // (XH * Y * 2)
-    RA = FB // 16 * 6 // 9 * 16
+    RA = FB // 16 * 4 // 9 * 16
     CB = CH // (Z * XL)
     nface, nband = XH * Y * 2, Z * XL
     face, band = lax.axis_index("face"), lax.axis_index("band")
@@ -538,7 +538,7 @@
     XH, Y, Z, XL = dims
     NX, HL = XH * XL, CH // XL
     FB, CB = 9 * CH // (XH * Y * 2), CH // (Z * XL)
-    RA = FB // 16 * 6 // 9 * 16
+    RA = FB // 16 * 4 // 9 * 16
     RB = FB - RA
     FP = -(-FB // 128) * 128
     hbm, vmem = pl.BlockSpec(memory_space=pltpu.HBM), pl.BlockSpec(memory_space=pltpu.VMEM)

time: 39.6 us -> 38.8 us (0.980)
  Pallas kernels: 38.9 us -> 38.1 us
    pallas_call x1, Pallas kernels: 38.1 us -> 37.2 us  [local(): pl.pallas_call(functools.partial(kernel, dims), out_shape=shapes, in_spec...]
where the time goes in v7:
time: 38.8 us; the launch traced here: 38.7 us
  Pallas kernels  38.1 us (98%)
  between operations  0.64 us (2%)
    pallas_call x1, Pallas kernels, local(): pl.pallas_call(functools.partial(kernel, dims), out_shape=shapes, in_spec...  37.2 us
    pallas_call x1, Pallas kernels, local(): pl.pallas_call(deliver, out_shape=shapes, in_specs=[vmem] * 4, out_specs=...  0.81 us

profile of v7, /device:TPU:1, one launch (start us, length us, event | category | flops | bytes accessed | tf_op | source)
XLA Modules:
  0.0 38.7 jit_solution(17440120242599766976)
XLA Ops:
  0.6 37.2 %shard_map.84 = (bf16[24,32,256]{2,1,0:T(8,128)(2,1)S(1)}, bf16[192,256]{1,0:T(8,128)(2,1)S(1)}, f32[16,144]{1,0:T(8,128)S(1)}, f32[16,144]{1,0:T(8,128)S(1)}) custom-call(bf16[12,16,256]{2,1,0:T(8,128)(2,1)} %coarse_h.1, bf16[24,32,256]{2,1,0:T(8,128)(2,1)} %skip_h.1, bf16[2304,256]{1,0:T(8,128)(2,1)} %bitcast.5, bf16[2304,256]{1,0:T(8,128)(2,1)} %bitcast.6, ...), custom_call_target="tpu_custom_call" | custom-call | tf_op jit(solution)/shard_map/pallas_call | solution.py:573
  37.9 0.8 %shard_map.85 = (bf16[24,32,256]{2,1,0:T(8,128)(2,1)}, bf16[192,256]{1,0:T(8,128)(2,1)}, f32[16,144]{1,0:T(8,128)}, f32[16,144]{1,0:T(8,128)}) custom-call(bf16[24,32,256]{2,1,0:T(8,128)(2,1)S(1)} %get-tuple-element.12.refs_0_, bf16[192,256]{1,0:T(8,128)(2,1)S(1)} %get-tuple-element.13.refs_1_, f32[16,144]{1,0:T(8,128)S(1)} %get-tuple-element.14.refs_2_, ...), custom_call_target="tpu_custom_call" | custom-call | tf_op jit(solution)/shard_map/pallas_call | solution.py:583
